TPU v7x, 128 devices: a whole 4x4x4 slice. The times are simulated.
128 devices in a mesh: ctx: 8 (over y, core), tp: 8 (over x_lo, z), pp: 2 (over x_hi).
Axes of the slice: x: 4 (x_hi: 2, x_lo: 2; x = x_hi * 2 + x_lo), y: 4, z: 4, core: 2. Of those that a mesh axis runs over, the one named last changes fastest.
Arguments:
- queries: bfloat16 [2, 2048, 12288], P('pp', 'ctx', 'tp'), may hold values from -8 to 8
- latents: bfloat16 [2, 2048, 576], P('pp', ('ctx', 'tp')), may hold values from -8 to 8
- latent_gain: float32 [2, 512], P('pp'), may hold values from 0.5 to 2
- w_ukv: bfloat16 [2, 512, 16384], P('pp', None, 'tp'), may hold values from -0.25 to 0.25
- w_o: bfloat16 [2, 8192, 7168], P('pp', 'tp'), may hold values from -0.1875 to 0.1875
- residual: bfloat16 [2, 2048, 7168], P('pp', ('ctx', 'tp')), may hold values from -3 to 3
- block_order: int32 [2, 16], P('pp'), may hold values from 0 to 15, each once within a row
Outputs:
- handed: bfloat16 [2, 2048, 7168], P('pp', ('ctx', 'tp'))
Inputs may be any that keep to these rules, and one draw needn't show every extreme that they name: `block_order`: each row names each of the 16 sequence blocks once.
All inputs are finite; a program needn't handle non-finite values.
Results may differ from a plain program's by a relative error of at most 0.02.
Values may be sent and summed in bfloat16 or wider, within the bound.
A program may use at most 128 MiB of HBM per device.

v0:
```python
import jax
import jax.numpy as jnp
from jax import lax
from jax.sharding import PartitionSpec as P

NOPE = 128
ROPE = 64
VDIM = 128
LATENT = 512


score_scale = 0.135


def passed_along(value, axis, steps):
    count = lax.axis_size(axis)
    pairs = [(source, (source + steps) % count) for source in range(count)]
    return lax.ppermute(value, axis, pairs)


def rotate(values, places):
    middle = values.shape[-1] // 2
    freqs = 10000.0 ** (-(jnp.arange(middle).astype(jnp.float32) * 2.0 / values.shape[-1]))
    angles = places[..., None] * freqs
    first_half = values[..., :middle]
    second_half = values[..., middle:]
    return jnp.concatenate(
        [
            first_half * jnp.cos(angles) - second_half * jnp.sin(angles),
            first_half * jnp.sin(angles) + second_half * jnp.cos(angles),
        ],
        axis=-1,
    )


def place_rows(order_row, first, count, block_len):
    row_ids = first + jnp.arange(count, dtype=jnp.int32)
    owners = row_ids // block_len
    table = jnp.arange(order_row.shape[0], dtype=jnp.int32)
    base = jnp.sum(jnp.where(owners[:, None] == table[None, :], order_row[None, :], 0), axis=1)
    return base * block_len + row_ids % block_len


def local(queries, latents, latent_gain, w_ukv, w_o, residual, block_order):
    order_row = block_order[0]
    tp_count = lax.axis_size("tp")
    tok_dev = queries.shape[1]
    block_len = tok_dev // 2
    lat_rows = latents.shape[1]
    heads_here = w_o.shape[1] // VDIM
    query_places = place_rows(order_row, lax.axis_index("ctx") * tok_dev, tok_dev, block_len)
    query_all = queries[0].reshape(tok_dev, heads_here, NOPE + ROPE)
    query_nope = query_all[..., :NOPE]
    query_rope = rotate(
        query_all[..., NOPE:].astype(jnp.float32), query_places.astype(jnp.float32)[:, None]
    ).astype(jnp.bfloat16)
    own_first = (lax.axis_index("ctx") * tp_count + lax.axis_index("tp")) * lat_rows
    own_places = place_rows(order_row, own_first, lat_rows, block_len)
    latent_rows = latents[0].astype(jnp.float32)
    compressed = latent_rows[:, :LATENT]
    scale_rows = lax.rsqrt(jnp.mean(compressed * compressed, axis=-1, keepdims=True) + 1e-06)
    normed = (compressed * scale_rows * latent_gain[0][None, :]).astype(jnp.bfloat16)
    own_rope = rotate(latent_rows[:, LATENT:], own_places.astype(jnp.float32)).astype(jnp.bfloat16)
    own_keys = jnp.concatenate([normed, own_rope], axis=-1)
    up_weights = w_ukv[0]

    def expand(latent_part):
        produced = jnp.dot(latent_part, up_weights, preferred_element_type=jnp.float32).astype(
            jnp.bfloat16
        )
        return produced.reshape(latent_part.shape[0], heads_here, NOPE + VDIM)

    piece = lax.all_gather(own_keys, ("ctx", "tp"), axis=0, tiled=True)
    make_keys = lambda: (expand(piece[:, :LATENT]), piece[:, LATENT:])
    key_places = place_rows(order_row, jnp.int32(0), piece.shape[0], block_len)
    running_max = jnp.full((tok_dev, heads_here), -1e30, jnp.float32)
    key_value, key_rope = make_keys()
    scores = (
        jnp.einsum(
            "thd,nhd->thn", query_nope, key_value[..., :NOPE], preferred_element_type=jnp.float32
        )
        + jnp.einsum("thr,nr->thn", query_rope, key_rope, preferred_element_type=jnp.float32)
    ) * score_scale
    allowed = (key_places[None, :] <= query_places[:, None])[:, None, :]
    scores = jnp.where(allowed, scores, -1e30)
    new_max = jnp.maximum(running_max, jnp.max(scores, axis=-1))
    weights = jnp.where(allowed, jnp.exp(scores - new_max[..., None]), 0.0)
    new_total = jnp.sum(weights, axis=-1)
    new_sum = jnp.einsum(
        "thn,nhd->thd",
        weights.astype(jnp.bfloat16),
        key_value[..., NOPE:],
        preferred_element_type=jnp.float32,
    )
    attention = (
        (new_sum / new_total[..., None]).astype(jnp.bfloat16).reshape(tok_dev, heads_here * VDIM)
    )
    out_weights = w_o[0]
    summed = lax.psum_scatter(
        jnp.dot(attention, out_weights, preferred_element_type=jnp.float32).astype(jnp.bfloat16),
        "tp",
        scatter_dimension=0,
        tiled=True,
    ).astype(jnp.float32)
    mixed = (summed + residual[0].astype(jnp.float32)).astype(jnp.bfloat16)
    handed = passed_along(mixed, "pp", 1)
    return handed[None]


def solution(mesh):
    in_specs = (
        P("pp", "ctx", "tp"),
        P("pp", ("ctx", "tp"), None),
        P("pp", None),
        P("pp", None, "tp"),
        P("pp", "tp", None),
        P("pp", ("ctx", "tp"), None),
        P("pp", None),
    )
    out_specs = P("pp", ("ctx", "tp"), None)
    return jax.shard_map(local, mesh=mesh, in_specs=in_specs, out_specs=out_specs, check_vma=False)
```

profile of v0, /device:TPU:0, one launch (start us, length us, event | category | flops | bytes accessed | tf_op | source)
XLA Modules:
  0.0 292.4 jit_solution(18152602769886171369)
XLA Ops:
  6.6 0.9 bitcast_convert_fusion
  7.5 0.7 select_reduce_fusion.2
  8.3 0.1 multiply_reduce_fusion
  8.4 0.1 fusion.38
  8.5 0.8 multiply_convert_fusion
  9.3 0.7 pad_maximum_fusion
  10.0 0.0 all-gather.2.cloned.1.call-update
  10.0 0.0 reduce-scatter.2.cloned.1.call-start
  10.1 1.4 copy.26
  11.5 0.8 select_reduce_fusion.1
  12.3 0.8 select_reduce_fusion
  13.1 0.2 multiply_cosine_fusion
  13.3 0.8 subtract_convert_fusion
  14.1 0.4 broadcast_compare_fusion
  14.5 155.7 %all-gather.2.cloned.1.call-done = bf16[2048,576]{1,0:T(8,128)(2,1)} async-done(((bf16[32,576]{1,0:T(8,128)(2,1)}), bf16[2048,576]{1,0:T(8,128)(2,1)}) %all-gather.2.cloned.1.call-update) | async-done | bytes 2359312 | tf_op jit(solution)/shard_map/all_gather | solution.py:73
  170.2 0.0 copy-done
  170.2 8.3 %convolution_convert_fusion = bf16[2048,2048]{0,1:T(8,128)(2,1)} fusion(bf16[2048,576]{1,0:T(8,128)(2,1)} %all-gather.2.cloned.1.call-done, bf16[1,512,2048]{2,1,0:T(8,128)(2,1)S(1)} %copy-done), kind=kOutput, calls=%fused_computation.13 | convolution fusion | flops 4299161600 | bytes 12582912 | tf_op jit(solution)/shard_map/dot_general | solution.py:68
  178.6 4.7 %fusion.14 = f32[8,2048,256]{2,1,0:T(8,128)S(1)} fusion(bf16[2048,8,256]{0,2,1:T(8,128)(2,1)} %bitcast.39, bf16[256,8,192]{0,2,1:T(8,128)(2,1)} %bitcast.38), kind=kOutput, calls=%fused_computation.14 | convolution fusion | flops 1073741824 | bytes 21495808 | tf_op jit(solution)/shard_map/thd,nhd->thn/dot_general | solution.py:79
  183.3 0.0 copy-done.3
  183.3 0.0 copy-done.4
  183.3 8.8 %fusion.57 = (f32[256,8]{0,1:T(8,128)S(1)}, f32[256,8,2048]{0,2,1:T(8,128)}) fusion(bf16[256,8,32]{0,2,1:T(8,128)(2,1)S(1)} %copy-done.4, bf16[256,8,32]{0,2,1:T(8,128)(2,1)S(1)} %copy-done.3, bf16[2048,576]{1,0:T(8,128)(2,1)} %all-gather.2.cloned.1.call-done, f32[8,2048,256]{2,1,0:T(8,128)S(1)} %fusion.14, pred[256,2048]{0,1:T(8,128)(4,1)S(1)} %broadcast_compare_fusion), kind=kOutput, calls=%fused_computation.89 | convolution fusion | flops 554170368 | bytes 34873344 | tf_op jit(solution)/shard_map/thr,nr->thn/dot_general | solution.py:82
  192.1 8.6 %fusion.4 = f32[256,8]{0,1:T(8,128)S(1)} fusion(f32[256,8,2048]{0,2,1:T(8,128)} %get-tuple-element.14, f32[256,8]{0,1:T(8,128)S(1)} %broadcast_maximum_fusion, pred[256,2048]{0,1:T(8,128)(4,1)S(1)} %broadcast_compare_fusion), kind=kLoop, calls=%fused_computation.6 | loop fusion | flops 12580864 | bytes 17317888 | tf_op jit(solution)/shard_map/reduce_sum | solution.py:88
  200.8 10.1 %divide_convert_fusion = bf16[256,8,128]{0,2,1:T(8,128)(2,1)S(1)} fusion(f32[256,8,2048]{0,2,1:T(8,128)} %get-tuple-element.14, f32[256,8]{0,1:T(8,128)S(1)} %broadcast_maximum_fusion, pred[256,2048]{0,1:T(8,128)(4,1)S(1)} %broadcast_compare_fusion, bf16[2048,8,256]{0,2,1:T(8,128)(2,1)} %bitcast.40, f32[256,8]{0,1:T(8,128)S(1)} %fusion.4), kind=kOutput, calls=%fused_computation.20 | convolution fusion | flops 1086849024 | bytes 22036480 | tf_op jit(solution)/shard_map/thn,nhd->thd/dot_general | solution.py:89
  210.9 0.0 copy-start.1
  210.9 0.0 copy-start.5
  210.9 11.0 %fusion.6 = bf16[256,7168]{1,0:T(8,128)(2,1)} fusion(bf16[256,1024]{0,1:T(8,128)(2,1)S(1)} %bitcast.41, bf16[1,1024,7168]{2,1,0:T(8,128)(2,1)} %param.11), kind=kOutput, calls=%fused_computation.8 | convolution fusion | flops 3759931392 | bytes 18874368 | tf_op jit(solution)/shard_map/dot_general | solution.py:100
  221.8 0.0 reduce-scatter.2.cloned.1.call-update
  221.9 49.7 %reduce-scatter.2.cloned.1.call-done = bf16[32,7168]{1,0:T(8,128)(2,1)} async-done(((bf16[256,7168]{1,0:T(8,128)(2,1)}), bf16[32,7168]{1,0:T(8,128)(2,1)}) %reduce-scatter.2.cloned.1.call-update) | async-done | bytes 458768 | tf_op jit(solution)/shard_map/reduce_scatter | solution.py:99
  271.6 1.1 fusion.28
  272.7 2.7 collective-permute-start
  275.4 9.4 %collective-permute-done = bf16[32,7168]{1,0:T(8,128)(2,1)S(1)} collective-permute-done((bf16[32,7168]{1,0:T(8,128)(2,1)S(1)}, bf16[32,7168]{1,0:T(8,128)(2,1)S(1)}, u32[]{:S(2)}, u32[]{:S(2)}) %collective-permute-start) | collective-permute-done | bytes 458784 | tf_op jit(solution)/shard_map/ppermute | solution.py:18
  284.8 0.8 copy.37
  (18 shorter events, 0.1 us)
Async XLA Ops:
  6.5 163.7 %copy-start = (bf16[1,512,2048]{2,1,0:T(8,128)(2,1)S(1)}, bf16[1,512,2048]{2,1,0:T(8,128)(2,1)}, u32[]{:S(2)}) copy-start(bf16[1,512,2048]{2,1,0:T(8,128)(2,1)} %param.10) | copy-start | bytes 6291460
  6.5 163.7 %all-gather.2.cloned.1.call-start = ((), (), s32[]{:S(2)}) async-start(), calls=%async_computation.1 | async-start | bytes 2662400 | tf_op jit(solution)/shard_map/all_gather | solution.py:73
  10.0 261.6 %reduce-scatter.2.cloned.1.call-start = ((), (), s32[]{:S(2)}) async-start(), calls=%async_computation.2 | async-start | bytes 4128768 | tf_op jit(solution)/shard_map/reduce_scatter | solution.py:99
  11.5 167.1 %copy-start.2 = (bf16[1,256,1536]{1,2,0:T(8,128)(2,1)}, bf16[1,256,1536]{1,2,0:T(8,128)(2,1)S(1)}, u32[]{:S(2)}) copy-start(bf16[1,256,1536]{1,2,0:T(8,128)(2,1)S(1)} %copy.26) | copy-start | bytes 2359300
  178.5 4.7 %copy-start.3 = (bf16[256,8,32]{0,2,1:T(8,128)(2,1)S(1)}, bf16[256,8,32]{0,2,1:T(8,128)(2,1)}, u32[]{:S(2)}) copy-start(bf16[256,8,32]{0,2,1:T(8,128)(2,1)} %get-tuple-element.7) | copy-start | bytes 393220
  178.6 4.7 %copy-start.4 = (bf16[256,8,32]{0,2,1:T(8,128)(2,1)S(1)}, bf16[256,8,32]{0,2,1:T(8,128)(2,1)}, u32[]{:S(2)}) copy-start(bf16[256,8,32]{0,2,1:T(8,128)(2,1)} %get-tuple-element.8) | copy-start | bytes 393220
  210.9 74.7 %copy-start.1 = (bf16[1,512,2048]{2,1,0:T(8,128)(2,1)S(1)}, bf16[1,512,2048]{2,1,0:T(8,128)(2,1)}, u32[]{:S(2)}) copy-start(bf16[1,512,2048]{2,1,0:T(8,128)(2,1)} %param.10) | copy-start | bytes 6291460
  210.9 60.7 %copy-start.5 = (bf16[1,32,7168]{2,1,0:T(8,128)(2,1)S(1)}, bf16[1,32,7168]{2,1,0:T(8,128)(2,1)}, u32[]{:S(2)}) copy-start(bf16[1,32,7168]{2,1,0:T(8,128)(2,1)} %param.12) | copy-start | bytes 1376260
  272.7 12.1 %collective-permute-start = (bf16[32,7168]{1,0:T(8,128)(2,1)S(1)}, bf16[32,7168]{1,0:T(8,128)(2,1)S(1)}, u32[]{:S(2)}, u32[]{:S(2)}) collective-permute-start(bf16[32,7168]{1,0:T(8,128)(2,1)S(1)} %fusion.28), channel_id=1, source_target_pairs={{0,1},{1,0},{2,3},{3,2},{4,5},{5,4},{6,7},{7,6},{8,9},{9,8},{10,11... | collective-permute-start | bytes 1376264 | tf_op jit(solution)/shard_map/ppermute | solution.py:18
Sparse Core Ops, SparseCore 0:
  10.1 160.0 all-gather.1
  222.0 49.5 reduce-scatter.1
where the time goes:
time: 293 us; the launch traced here: 292 us
  waiting for transfers between devices  215 us (73%)
  matrix products  42.9 us (15%)
  other arithmetic  16.2 us (6%)
  between operations  13.5 us (5%)
    all_gather x1, waiting for transfers between devices, local(): piece = lax.all_gather(own_keys, ('ctx', 'tp'), axis=0, tiled=True)  156 us
    reduce_scatter x1, waiting for transfers between devices, local(): lax.psum_scatter(jnp.dot(attention, out_weights, preferred_element_type=j...  49.7 us
    dot_general x1, matrix products, local(): jnp.dot(attention, out_weights, preferred_element_type=jnp.float32)  11 us
    dot_general x1, matrix products, local(): jnp.einsum('thn,nhd->thd', weights.astype(jnp.bfloat16), key_value[..., N...  10.1 us
    ppermute x1, waiting for transfers between devices, passed_along(): return lax.ppermute(value, axis, pairs)  9.41 us
    dot_general x1, matrix products, local(): jnp.einsum('thr,nr->thn', query_rope, key_rope, preferred_element_type=jn...  8.81 us
    reduce_sum x1, other arithmetic, local(): new_total = jnp.sum(weights, axis=-1)  8.63 us
    dot_general x1, matrix products, expand(): jnp.dot(latent_part, up_weights, preferred_element_type=jnp.float32)  8.34 us
  transfers between devices with their start and end apart: 3, of which 3 were waited for; matrix products, arithmetic and copies ran while one was open for 2% of the time, Pallas kernels for 0%

commit v1 on v0

v1 whole, which is shorter than its diff:
```python
import functools
import math

import jax
import jax.numpy as jnp
import numpy as np
from jax import lax
from jax.experimental import pallas as pl
from jax.experimental.pallas import tpu as pltpu
from jax.sharding import PartitionSpec as P

NOPE = 128
ROPE = 64
VDIM = 128
LATENT = 512
BLOCK = 128
HEADS_HERE = 8
ROWS = 256
KEYS = 2048
LATROWS = 32
D = 7168
KW = LATENT + 128
PIECE = 1024
HALF = PIECE // 2
PIECES = ("z", "x", "z", "x", "z", "x", "z")
SCALE2 = 0.135 * math.log2(math.e)

MESH = pl.DeviceIdType.MESH


def position():
    c = lax.axis_index("ctx")
    t = lax.axis_index("tp")
    p = lax.axis_index("pp")
    return c // 2, lax.rem(c, 2), t // 4, lax.rem(t, 4), p


def device(y, k, a, z, p):
    return (y * 2 + k, a * 4 + z, p)


def turn(v, n):
    return lax.rem(v + n, 4)


def rope_tables():
    f = 10000.0 ** (-(np.arange(32, dtype=np.float64) * 2.0 / ROPE))
    lane_f = np.tile(f, 4)
    sign = np.tile(np.concatenate([-np.ones(32), np.ones(32)]), 2)
    inner = np.arange(BLOCK, dtype=np.float64)[:, None] * lane_f
    outer = np.arange(16, dtype=np.float64)[:, None] * BLOCK * lane_f
    within = np.stack([np.cos(inner), np.sin(inner) * sign]).astype(np.float32)
    blocks = np.stack([np.cos(outer), np.sin(outer) * sign]).astype(np.float32)
    return within, blocks


def rotation(within, blocks, which, first, count):
    c_in = within[0, pl.ds(first, count), :]
    s_in = within[1, pl.ds(first, count), :]
    c_out = blocks[0, pl.ds(which, 1), :]
    s_out = blocks[1, pl.ds(which, 1), :]
    return c_out * c_in - s_out * s_in, s_out * c_in + c_out * s_in


def swapped(v):
    return jnp.concatenate([v[:, 32:64], v[:, :32], v[:, 96:], v[:, 64:96]], axis=1)


def remote(src, dst, send, recv, to):
    return pltpu.make_async_remote_copy(
        src_ref=src, dst_ref=dst, send_sem=send, recv_sem=recv, device_id=to, device_id_type=MESH
    )


def gather_kernel(order, lat, gain, q, within, blocks, kl, qcat, send, recv):
    y, k, a, z, p = position()
    c = y * 2 + k
    z_to = [device(y, k, a, turn(z, n), p) for n in (1, 3, 2)]
    y_to = [device(turn(y, n), k, a, z, p) for n in (1, 3, 2)]
    x_to = device(y, k, 1 - a, z, p)
    k_to = device(y, 1 - k, a, z, p)
    barrier = pltpu.get_barrier_semaphore()
    for to in z_to + y_to + [x_to, k_to]:
        pl.semaphore_signal(barrier, inc=1, device_id=to, device_id_type=MESH)

    rows = lat[0].astype(jnp.float32)
    part = rows[:, :LATENT]
    scale = lax.rsqrt(jnp.mean(part * part, axis=-1, keepdims=True) + 1e-6)
    normed = (part * scale * gain[...]).astype(jnp.bfloat16)
    tail = rows[:, LATENT:]
    twice = jnp.concatenate([tail, tail], axis=1)
    cos, sin = rotation(within, blocks, order[0, c * 2 + a], z * LATROWS, LATROWS)
    roped = (twice * cos + swapped(twice) * sin).astype(jnp.bfloat16)
    own = jnp.concatenate([normed, roped], axis=1)
    kl[0, y, k, a, z] = own[:16]
    kl[1, y, k, a, z] = own[16:]
    pl.semaphore_wait(barrier, 8)

    def copy(view, to, n):
        made = remote(view, view, send.at[n], recv.at[n], to)
        made.start()
        return made

    first = copy(kl.at[:, y, k, a, z], x_to, 0)

    places = [order[0, c * 2], order[0, c * 2 + 1]]
    lane = lax.broadcasted_iota(jnp.int32, (BLOCK, 128), 1)
    for half in range(2):
        cos, sin = rotation(within, blocks, places[half], 0, BLOCK)
        at = pl.ds(half * BLOCK, BLOCK)
        for pair in range(HEADS_HERE // 2):
            both = q[0, at, pair * 384 : (pair + 1) * 384].astype(jnp.float32)
            v = jnp.concatenate([both[:, 128:192], both[:, 320:384]], axis=1)
            turned = v * cos + swapped(v) * sin
            low = jnp.where(lane < ROPE, turned, 0.0)
            high = jnp.where(lane < ROPE, 0.0, turned)
            qcat[pair * 2, at, :] = jnp.concatenate([both[:, :128], low], axis=1).astype(jnp.bfloat16)
            qcat[pair * 2 + 1, at, :] = jnp.concatenate([both[:, 192:320], high], axis=1).astype(
                jnp.bfloat16
            )

    first.wait_recv()
    second = [copy(kl.at[0, y, k, :, z], to, 1 + i) for i, to in enumerate(z_to)]
    second += [copy(kl.at[1, y, k, :, z], to, 4 + i) for i, to in enumerate(y_to)]
    for made in second[:3]:
        made.wait_recv()
    third = [copy(kl.at[0, y, k], to, 7 + i) for i, to in enumerate(y_to)]
    for made in second[3:]:
        made.wait_recv()
    third += [copy(kl.at[1, :, k, :, z], to, 10 + i) for i, to in enumerate(z_to)]
    over = [copy(kl.at[0, y, k], k_to, 13), copy(kl.at[1, :, k, :, z], k_to, 14)]
    for i, n in enumerate((3, 1, 2)):
        third[i].wait_recv()
        over.append(copy(kl.at[0, turn(y, n), k], k_to, 15 + i))
        third[3 + i].wait_recv()
        over.append(copy(kl.at[1, :, k, :, turn(z, n)], k_to, 18 + i))
    for made in over:
        made.wait_recv()
    for made in [first] + second + third + over:
        made.wait_send()


def gather(latents, gain, queries, order):
    within, blocks = rope_tables()
    vmem = pl.BlockSpec(memory_space=pltpu.VMEM)
    return pl.pallas_call(
        gather_kernel,
        out_shape=[
            jax.ShapeDtypeStruct((2, 4, 2, 2, 4, 16, KW), jnp.bfloat16),
            jax.ShapeDtypeStruct((HEADS_HERE, ROWS, 256), jnp.bfloat16),
        ],
        in_specs=[pl.BlockSpec(memory_space=pltpu.SMEM)] + [vmem] * 5,
        out_specs=[vmem, vmem],
        scratch_shapes=[pltpu.SemaphoreType.DMA((21,)), pltpu.SemaphoreType.DMA((21,))],
        compiler_params=pltpu.CompilerParams(
            collective_id=0, has_side_effects=True, vmem_limit_bytes=24 * 2**20
        ),
        name="gather",
    )(order, latents, gain, queries, jnp.asarray(within), jnp.asarray(blocks))


def attend_kernel(order, kl, qcat, w, out):
    c = lax.axis_index("ctx")
    spot = lax.broadcasted_iota(jnp.int32, (1, 128), 1)
    inside = (lax.rem(spot, 64) // 16) * 32 + lax.rem(spot, 16)
    groups = []
    for half in range(2):
        for pair in range(8):
            base = jnp.where(spot < 64, order[0, pair * 2], order[0, pair * 2 + 1])
            groups.append(base * BLOCK + half * 16 + inside)
    key_at = jnp.concatenate(groups, axis=1)
    row = lax.broadcasted_iota(jnp.int32, (ROWS, 1), 0)
    base = jnp.where(row < BLOCK, order[0, c * 2], order[0, c * 2 + 1])
    query_at = base * BLOCK + lax.rem(row, BLOCK)
    allowed = key_at <= query_at
    for h in range(2):
        kv = jnp.dot(
            kl[:, :LATENT], w[0, :, h * 256 : (h + 1) * 256], preferred_element_type=jnp.float32
        ).astype(jnp.bfloat16)
        key = jnp.concatenate([kv[:, :NOPE], kl[:, LATENT:]], axis=1)
        scores = lax.dot_general(
            qcat[h], key, (((1,), (1,)), ((), ())), preferred_element_type=jnp.float32
        )
        scores = jnp.where(allowed, scores * SCALE2, -1e30)
        top = jnp.max(scores, axis=-1, keepdims=True)
        weights = jnp.exp2(scores - top)
        total = jnp.sum(weights, axis=-1, keepdims=True)
        summed = jnp.dot(
            weights.astype(jnp.bfloat16), kv[:, NOPE:], preferred_element_type=jnp.float32
        )
        out[:, h * VDIM : (h + 1) * VDIM] = (summed / total).astype(jnp.bfloat16)


def attend(order, kl, qcat, w):
    return pl.pallas_call(
        attend_kernel,
        grid=(HEADS_HERE // 2,),
        out_shape=jax.ShapeDtypeStruct((ROWS, HEADS_HERE * VDIM), jnp.bfloat16),
        in_specs=[
            pl.BlockSpec(memory_space=pltpu.SMEM),
            pl.BlockSpec((KEYS, KW), lambda i: (0, 0)),
            pl.BlockSpec((2, ROWS, 256), lambda i: (i, 0, 0)),
            pl.BlockSpec((1, LATENT, 512), lambda i: (0, 0, i)),
        ],
        out_specs=pl.BlockSpec((ROWS, 2 * VDIM), lambda i: (0, i)),
        compiler_params=pltpu.CompilerParams(vmem_limit_bytes=40 * 2**20),
        name="attend",
    )(order, kl.reshape(KEYS, KW), qcat, w)


def project_kernel(att, w, residual, out, wv, part, early, late, crossed, final, wsem, send, recv):
    y, k, a, z, p = position()
    up, down, far = turn(z, 1), turn(z, 3), turn(z, 2)
    to_up, to_down = device(y, k, a, up, p), device(y, k, a, down, p)
    to_x = device(y, k, 1 - a, z, p)
    to_pp = device(y, k, 1 - a, z, 1 - p)
    barrier = pltpu.get_barrier_semaphore()
    for to in (to_up, to_down, to_x, to_pp):
        pl.semaphore_signal(barrier, inc=1, device_id=to, device_id_type=MESH)
    columns = [pl.ds(j * PIECE, PIECE) for j in range(len(PIECES))]
    loads = []
    for j in range(len(PIECES)):
        load = pltpu.make_async_copy(w.at[0, :, columns[j]], wv.at[j], wsem.at[j])
        load.start()
        loads.append(load)
    left, right = pl.ds(0, HALF), pl.ds(HALF, HALF)
    sent = []
    copies = {}

    def copy(src, dst, j, n, to):
        made = remote(src, dst, send.at[j, n], recv.at[j, n], to)
        made.start()
        sent.append(made)
        copies[j, n] = made

    def wide(ref):
        return ref[...].astype(jnp.float32)

    def own_residual(j):
        return residual[0, :, columns[j]].astype(jnp.float32)

    def spread(j, side):
        copy(part.at[j, side, far, :, left], early.at[j, 0, side], j, 0, to_up)
        copy(part.at[j, side, far, :, right], early.at[j, 1, side], j, 1, to_down)
        copy(part.at[j, side, up, :, right], late.at[j, 0, side, :, right], j, 2, to_up)
        copy(part.at[j, side, down, :, left], late.at[j, 1, side, :, left], j, 3, to_down)

    def relay(j, side):
        copies[j, 0].wait_recv()
        mine = part.at[j, side, up, :, left]
        mine[...] = (wide(mine) + wide(early.at[j, 0, side])).astype(jnp.bfloat16)
        copy(mine, late.at[j, 0, side, :, left], j, 4, to_up)
        copies[j, 1].wait_recv()
        mine = part.at[j, side, down, :, right]
        mine[...] = (wide(mine) + wide(early.at[j, 1, side])).astype(jnp.bfloat16)
        copy(mine, late.at[j, 1, side, :, right], j, 5, to_down)

    def landed(j):
        for n in (2, 3, 4, 5):
            copies[j, n].wait_recv()

    def ring_sum(j, side):
        return wide(part.at[j, side, z]) + wide(late.at[j, 0, side]) + wide(late.at[j, 1, side])

    def finish(j, value):
        final[j] = value.astype(jnp.bfloat16)
        copy(final.at[j], out.at[0, :, columns[j]], j, 7, to_pp)

    def product(j):
        loads[j].wait()
        made = jnp.dot(att[...], wv[j], preferred_element_type=jnp.float32)
        part[j] = made.astype(jnp.bfloat16).reshape(2, 4, LATROWS, PIECE)

    def z_step(j, step):
        if step == 0:
            product(j)
            if j == 0:
                pl.semaphore_wait(barrier, 4)
            spread(j, slice(None))
        elif step == 1:
            relay(j, slice(None))
        elif step == 2:
            landed(j)
            part[j, a, z] = (ring_sum(j, a) + own_residual(j)).astype(jnp.bfloat16)
            copy(part.at[j, a, z], crossed.at[j, 0], j, 6, to_x)
        elif step == 3:
            copies[j, 6].wait_recv()
            finish(j, ring_sum(j, 1 - a) + wide(crossed.at[j, 0]))

    def x_step(j, step):
        if step == 0:
            product(j)
            part[j, a, z] = (wide(part.at[j, a, z]) + own_residual(j)).astype(jnp.bfloat16)
            copy(part.at[j, a], crossed.at[j], j, 6, to_x)
        elif step == 1:
            copies[j, 6].wait_recv()
            part[j, 1 - a] = (wide(part.at[j, 1 - a]) + wide(crossed.at[j])).astype(jnp.bfloat16)
            spread(j, 1 - a)
        elif step == 2:
            relay(j, 1 - a)
        elif step == 3:
            landed(j)
            finish(j, ring_sum(j, 1 - a))

    steps = {"z": z_step, "x": x_step}
    for step in range(len(PIECES) + 3):
        for j, kind in enumerate(PIECES):
            if 0 <= step - j < 4:
                steps[kind](j, step - j)
    for j in range(len(PIECES)):
        copies[j, 7].wait_recv()
    for made in sent:
        made.wait_send()


def project(att, w_o, residual):
    n = len(PIECES)
    vmem = pl.BlockSpec(memory_space=pltpu.VMEM)
    return pl.pallas_call(
        project_kernel,
        out_shape=jax.ShapeDtypeStruct((1, LATROWS, D), jnp.bfloat16),
        in_specs=[vmem, pl.BlockSpec(memory_space=pl.ANY), vmem],
        out_specs=vmem,
        scratch_shapes=[
            pltpu.VMEM((n, HEADS_HERE * VDIM, PIECE), jnp.bfloat16),
            pltpu.VMEM((n, 2, 4, LATROWS, PIECE), jnp.bfloat16),
            pltpu.VMEM((n, 2, 2, LATROWS, HALF), jnp.bfloat16),
            pltpu.VMEM((n, 2, 2, LATROWS, PIECE), jnp.bfloat16),
            pltpu.VMEM((n, 4, LATROWS, PIECE), jnp.bfloat16),
            pltpu.VMEM((n, LATROWS, PIECE), jnp.bfloat16),
            pltpu.SemaphoreType.DMA((n,)),
            pltpu.SemaphoreType.DMA((n, 8)),
            pltpu.SemaphoreType.DMA((n, 8)),
        ],
        compiler_params=pltpu.CompilerParams(
            collective_id=1, has_side_effects=True, vmem_limit_bytes=48 * 2**20
        ),
        name="project",
    )(att, w_o, residual)


def local(queries, latents, latent_gain, w_ukv, w_o, residual, block_order):
    kl, qcat = gather(latents, latent_gain, queries, block_order)
    att = attend(block_order, kl, qcat, w_ukv)
    return project(att, w_o, residual)


def solution(mesh):
    in_specs = (
        P("pp", "ctx", "tp"),
        P("pp", ("ctx", "tp"), None),
        P("pp", None),
        P("pp", None, "tp"),
        P("pp", "tp", None),
        P("pp", ("ctx", "tp"), None),
        P("pp", None),
    )
    out_specs = P("pp", ("ctx", "tp"), None)
    return jax.shard_map(local, mesh=mesh, in_specs=in_specs, out_specs=out_specs, check_vma=False)
```

time: 293 us -> 102 us (0.35)
  waiting for transfers between devices: 215 us -> 0 us
  Pallas kernels: 0 us -> 93.9 us
  matrix products: 42.9 us -> 0 us
  other arithmetic: 16.2 us -> 0 us
  between operations: 13.5 us -> 0.05 us
  local copies, waits for them, and re-layouts: 2.2 us -> 7.88 us
    all_gather x1 -> x0, waiting for transfers between devices: 156 us -> none  [local(): piece = lax.all_gather(own_keys, ('ctx', 'tp'), axis=0, tiled=True)]
    pallas_call x0 -> x3, Pallas kernels: none -> 93.9 us  [the longest x1 54.5 us: project(): pl.pallas_call(project_kernel, out_shape=jax.ShapeDtypeStruct((1, LATROWS...]
    reduce_scatter x1 -> x0, waiting for transfers between devices: 49.7 us -> none  [local(): lax.psum_scatter(jnp.dot(attention, out_weights, preferred_element_type=j...]
    dot_general x5 -> x0, matrix products: 42.9 us -> none  [the longest x1 11 us: local(): jnp.dot(attention, out_weights, preferred_element_type=jnp.float32)]
    reduce_sum x5 -> x0, other arithmetic: 11 us -> none  [the longest x1 8.63 us: local(): new_total = jnp.sum(weights, axis=-1)]
    ppermute x1 -> x0, waiting for transfers between devices: 9.41 us -> none  [passed_along(): return lax.ppermute(value, axis, pairs)]
    unnamed x14 -> x19, local copies, waits for them, and re-layouts: 2.2 us -> 7.88 us
  transfers between devices with their start and end apart: 3 -> 0, of which waited for: 3 -> 0; matrix products, arithmetic and copies ran while one was open for 2% -> 0% of each run, Pallas kernels for 0% -> 0%
where the time goes in v1:
time: 102 us
  Pallas kernels  93.9 us (92%)
  local copies, waits for them, and re-layouts  7.88 us (8%)
    pallas_call x1, Pallas kernels, project(): pl.pallas_call(project_kernel, out_shape=jax.ShapeDtypeStruct((1, LATROWS...  54.5 us
    pallas_call x1, Pallas kernels, gather(): pl.pallas_call(gather_kernel, out_shape=[jax.ShapeDtypeStruct((2, 4, 2, 2...  22.6 us
    pallas_call x1, Pallas kernels, attend(): pl.pallas_call(attend_kernel, grid=(HEADS_HERE // 2,), out_shape=jax.Shap...  16.8 us
    unnamed x19, local copies, waits for them, and re-layouts  7.88 us

profile of v1, /device:TPU:0, one launch (start us, length us, event | category | flops | bytes accessed | tf_op | source)
XLA Modules:
  0.0 101.8 jit_solution(7475814568759877550)
XLA Ops:
  0.0 0.0 copy-start.1
  0.0 1.1 %copy-done.1 = bf16[1,256,1536]{2,1,0:T(8,128)(2,1)S(1)} copy-done((bf16[1,256,1536]{2,1,0:T(8,128)(2,1)S(1)}, bf16[1,256,1536]{2,1,0:T(8,128)(2,1)}, u32[]{:S(2)}) %copy-start.1) | copy-done | bytes 786456
  1.1 0.0 copy-start.3
  1.1 0.9 copy-done.3
  2.0 0.0 copy-start.4
  2.0 0.8 copy-done.4
  2.8 0.0 copy-start.5
  2.8 0.7 copy-done.5
  3.5 0.0 copy-start.6
  3.5 0.7 copy-done.6
  4.2 0.0 copy-start.8
  4.2 0.7 copy-done.8
  4.9 22.6 %gather.1 = (bf16[2,4,2,2,4,16,640]{6,5,4,3,2,1,0:T(8,128)(2,1)S(1)}, bf16[8,256,256]{2,1,0:T(8,128)(2,1)S(1)}) custom-call(s32[1,16]{1,0:T(1,128)S(1)} %copy-done.6, bf16[1,32,576]{2,1,0:T(8,128)(2,1)S(1)} %copy-done.4, f32[1,512]{1,0:T(1,128)S(1)} %copy-done.8, bf16[1,256,1536]{2,1,0:T(8,128)(2,1)S(1)} %copy-done.1, f32[2,128,128]{2,1,0:T(8,128)S(1)} %copy-done.3, ...), custom_call_target="tpu_custom_call" | custom-call | tf_op jit(solution)/shard_map/gather/pallas_call | solution.py:146
  27.4 0.0 copy-start
  27.5 1.6 %copy-done = bf16[1,512,2048]{2,1,0:T(8,128)(2,1)S(1)} copy-done((bf16[1,512,2048]{2,1,0:T(8,128)(2,1)S(1)}, bf16[1,512,2048]{2,1,0:T(8,128)(2,1)}, u32[]{:S(2)}) %copy-start) | copy-done | bytes 2097176
  29.0 0.0 copy-start.7
  29.0 0.7 copy-done.7
  29.7 0.0 copy-start.2
  29.7 16.8 %attend.1.att = bf16[256,1024]{1,0:T(8,128)(2,1)S(1)} custom-call(s32[1,16]{1,0:T(1,128)S(1)} %copy-done.7, bf16[2048,640]{1,0:T(8,128)(2,1)S(1)} %bitcast.1, bf16[8,256,256]{2,1,0:T(8,128)(2,1)S(1)} %get-tuple-element.8.qcat, bf16[1,512,2048]{2,1,0:T(8,128)(2,1)S(1)} %copy-done), custom_call_target="tpu_custom_call" | custom-call | tf_op jit(solution)/shard_map/attend/pallas_call | solution.py:195
  46.5 0.0 copy-done.2
  46.5 54.5 %project.1 = bf16[1,32,7168]{2,1,0:T(8,128)(2,1)S(1)} custom-call(bf16[256,1024]{1,0:T(8,128)(2,1)S(1)} %attend.1.att, bf16[1,1024,7168]{2,1,0:T(8,128)(2,1)} %w.3, bf16[1,32,7168]{2,1,0:T(8,128)(2,1)S(1)} %copy-done.2), custom_call_target="tpu_custom_call" | custom-call | tf_op jit(solution)/shard_map/project/pallas_call | solution.py:319
  101.0 0.8 copy.11
Async XLA Ops:
  0.0 1.1 %copy-start.1 = (bf16[1,256,1536]{2,1,0:T(8,128)(2,1)S(1)}, bf16[1,256,1536]{2,1,0:T(8,128)(2,1)}, u32[]{:S(2)}) copy-start(bf16[1,256,1536]{2,1,0:T(8,128)(2,1)} %q.1) | copy-start | bytes 2359300
  1.1 0.9 copy-start.3
  2.0 0.8 copy-start.4
  2.8 0.7 copy-start.5
  3.5 0.7 copy-start.6
  4.2 0.7 copy-start.8
  27.4 1.6 %copy-start = (bf16[1,512,2048]{2,1,0:T(8,128)(2,1)S(1)}, bf16[1,512,2048]{2,1,0:T(8,128)(2,1)}, u32[]{:S(2)}) copy-start(bf16[1,512,2048]{2,1,0:T(8,128)(2,1)} %w.2) | copy-start | bytes 6291460
  29.0 0.7 copy-start.7
  29.7 16.8 %copy-start.2 = (bf16[1,32,7168]{2,1,0:T(8,128)(2,1)S(1)}, bf16[1,32,7168]{2,1,0:T(8,128)(2,1)}, u32[]{:S(2)}) copy-start(bf16[1,32,7168]{2,1,0:T(8,128)(2,1)} %residual.1) | copy-start | bytes 1376260

commit v2 on v1

v2 whole, which is shorter than its diff:
```python
import math

import jax
import jax.numpy as jnp
import numpy as np
from jax import lax
from jax.experimental import pallas as pl
from jax.experimental.pallas import tpu as pltpu
from jax.sharding import PartitionSpec as P

NOPE = 128
ROPE = 64
VDIM = 128
LATENT = 512
BLOCK = 128
HEADS = 8
ROWS = 256
LATROWS = 32
D = 7168
KW = LATENT + 128
CHUNK = 512
PIECE = 1024
HALF = PIECE // 2
PIECES = ("z", "x", "z", "x", "z", "x", "z")
SCALE2 = 0.135 * math.log2(math.e)

MESH = pl.DeviceIdType.MESH


def device(y, k, a, z, p):
    return (y * 2 + k, a * 4 + z, p)


def turn(v, n):
    return lax.rem(v + n, 4)


def rope_tables():
    f = 10000.0 ** (-(np.arange(32, dtype=np.float64) * 2.0 / ROPE))
    lane_f = np.tile(f, 4)
    sign = np.tile(np.concatenate([-np.ones(32), np.ones(32)]), 2)
    inner = np.arange(BLOCK, dtype=np.float64)[:, None] * lane_f
    outer = np.arange(16, dtype=np.float64)[:, None] * BLOCK * lane_f
    within = np.stack([np.cos(inner), np.sin(inner) * sign]).astype(np.float32)
    blocks = np.stack([np.cos(outer), np.sin(outer) * sign]).astype(np.float32)
    return np.concatenate([within, blocks], axis=1)


def rotation(tables, which, first, count):
    c_in = tables[0, pl.ds(first, count), :]
    s_in = tables[1, pl.ds(first, count), :]
    c_out = tables[0, pl.ds(BLOCK + which, 1), :]
    s_out = tables[1, pl.ds(BLOCK + which, 1), :]
    return c_out * c_in - s_out * s_in, s_out * c_in + c_out * s_in


def swapped(v):
    return jnp.concatenate([v[:, 32:64], v[:, :32], v[:, 96:], v[:, 64:96]], axis=1)


def remote(src, dst, send, recv, to):
    return pltpu.make_async_remote_copy(
        src_ref=src, dst_ref=dst, send_sem=send, recv_sem=recv, device_id=to, device_id_type=MESH
    )


def wide(ref):
    return ref[...].astype(jnp.float32)


def layer_kernel(
    lat_in, gain_in, tables_in, order_in, q_in, up_in, w_in, residual_in,
    out,
    lat, gain, tables, order, q, up, wv, residual,
    kl, qcat, top, acc, att,
    part, early, late, crossed, final,
    load_sem, up_sem, w_sem, g_send, g_recv, send, recv,
):
    c = lax.axis_index("ctx")
    t = lax.axis_index("tp")
    p = lax.axis_index("pp")
    y, k, a, z = c // 2, lax.rem(c, 2), t // 4, lax.rem(t, 4)
    z_to = {n: device(y, k, a, turn(z, n), p) for n in (1, 3, 2)}
    y_to = {n: device(turn(y, n), k, a, z, p) for n in (1, 3, 2)}
    x_to = device(y, k, 1 - a, z, p)
    k_to = device(y, 1 - k, a, z, p)
    pp_to = device(y, k, 1 - a, z, 1 - p)

    barrier = pltpu.get_barrier_semaphore()
    for to in [*z_to.values(), *y_to.values(), x_to, k_to, pp_to]:
        pl.semaphore_signal(barrier, inc=1, device_id=to, device_id_type=MESH)

    loads = {}

    def load(name, src, dst, sem):
        made = pltpu.make_async_copy(src, dst, sem)
        made.start()
        loads[name] = made

    load("lat", lat_in.at[0], lat, load_sem.at[0])
    load("order", order_in, order, load_sem.at[1])
    load("gain", gain_in, gain, load_sem.at[2])
    load("tables", tables_in, tables, load_sem.at[3])
    load("q", q_in.at[0], q, load_sem.at[4])
    for h in range(HEADS):
        load(("up", h), up_in.at[0, :, pl.ds(h * 256, 256)], up.at[h], up_sem.at[h])
    columns = [pl.ds(j * PIECE, PIECE) for j in range(len(PIECES))]
    for j in range(len(PIECES)):
        load(("w", j), w_in.at[0, :, columns[j]], wv.at[j], w_sem.at[j])
    load("residual", residual_in.at[0], residual, load_sem.at[5])

    for name in ("lat", "order", "gain", "tables"):
        loads[name].wait()
    rows = lat[...].astype(jnp.float32)
    low_rank = rows[:, :LATENT]
    scale = lax.rsqrt(jnp.mean(low_rank * low_rank, axis=-1, keepdims=True) + 1e-6)
    normed = (low_rank * scale * gain[...]).astype(jnp.bfloat16)
    twice = jnp.concatenate([rows[:, LATENT:], rows[:, LATENT:]], axis=1)
    cos, sin = rotation(tables, order[0, c * 2 + a], z * LATROWS, LATROWS)
    roped = (twice * cos + swapped(twice) * sin).astype(jnp.bfloat16)
    own = jnp.concatenate([normed, roped], axis=1)
    kl[0, 0, 0, 0, 0] = own[:16]
    kl[0, 1, 0, 0, 0] = own[16:]
    pl.semaphore_wait(barrier, 9)

    sent = []

    def push(src, dst, n, to):
        made = remote(src, dst, g_send.at[n], g_recv.at[n], to)
        made.start()
        sent.append(made)
        return made

    to_x = push(kl.at[0, :, 0, 0, 0], kl.at[0, :, 0, 1, 0], 0, x_to)

    loads["q"].wait()
    lane = lax.broadcasted_iota(jnp.int32, (BLOCK, 128), 1)
    for half in range(2):
        cos, sin = rotation(tables, order[0, c * 2 + half], 0, BLOCK)
        at = pl.ds(half * BLOCK, BLOCK)
        for pair in range(HEADS // 2):
            both = q[at, pair * 384 : (pair + 1) * 384].astype(jnp.float32)
            v = jnp.concatenate([both[:, 128:192], both[:, 320:384]], axis=1)
            turned = v * cos + swapped(v) * sin
            low = jnp.where(lane < ROPE, turned, 0.0)
            high = jnp.where(lane < ROPE, 0.0, turned)
            qcat[pair * 2, at, :] = jnp.concatenate([both[:, :128], low], axis=1).astype(jnp.bfloat16)
            qcat[pair * 2 + 1, at, :] = jnp.concatenate([both[:, 192:320], high], axis=1).astype(
                jnp.bfloat16
            )

    to_x.wait_recv()
    near = []
    for i, n in enumerate((1, 3, 2)):
        near.append(push(kl.at[0, 0, 0, :, 0], kl.at[0, 0, 0, :, 4 - n], 1 + i, z_to[n]))
        near.append(push(kl.at[0, 1, 0, :, 0], kl.at[0, 1, 0, :, 4 - n], 4 + i, y_to[n]))
    for made in near:
        made.wait_recv()
    arrivals = {}
    for i, n in enumerate((3, 1, 2)):
        arrivals[4 - n] = (
            push(kl.at[0, 0, 0], kl.at[4 - n, 0, 0], 7 + i, y_to[n]),
            push(kl.at[0, 1, 0], kl.at[4 - n, 1, 0], 10 + i, z_to[n]),
        )

    def share(slot):
        return push(kl.at[slot, :, 0], kl.at[slot, :, 1], 13 + slot, k_to)

    row = lax.broadcasted_iota(jnp.int32, (ROWS, 1), 0)
    base = jnp.where(row < BLOCK, order[0, c * 2], order[0, c * 2 + 1])
    query_at = base * BLOCK + lax.rem(row, BLOCK)
    spot = lax.broadcasted_iota(jnp.int32, (1, 128), 1)
    minor = lax.rem(spot, 64) // 16
    deep = lax.rem(spot, 16)

    def key_places(slot):
        groups = []
        for core in range(2):
            there = turn(y, slot) * 2 + (k if core == 0 else 1 - k)
            block = jnp.where(spot < 64, order[0, there * 2 + a], order[0, there * 2 + 1 - a])
            groups.append(block * BLOCK + lax.rem(minor + z, 4) * LATROWS + deep)
        for core in range(2):
            block = jnp.zeros_like(spot)
            for m in range(4):
                there = turn(y, m) * 2 + (k if core == 0 else 1 - k)
                here = jnp.where(spot < 64, order[0, there * 2 + a], order[0, there * 2 + 1 - a])
                block = jnp.where(minor == m, here, block)
            groups.append(block * BLOCK + turn(z, slot) * LATROWS + 16 + deep)
        return jnp.concatenate(groups, axis=1)

    ones = jnp.ones((CHUNK, VDIM), jnp.bfloat16)

    def attend(slot, first, last):
        allowed = key_places(slot) <= query_at

        def one(h):
            latent = kl[slot].reshape(CHUNK, KW)
            kv = jnp.dot(latent[:, :LATENT], up[h], preferred_element_type=jnp.float32)
            kv = kv.astype(jnp.bfloat16)
            key = jnp.concatenate([kv[:, :NOPE], latent[:, LATENT:]], axis=1)
            scores = lax.dot_general(
                qcat[h], key, (((1,), (1,)), ((), ())), preferred_element_type=jnp.float32
            )
            scores = jnp.where(allowed, scores * SCALE2, -1e30)
            high = jnp.max(scores, axis=-1, keepdims=True)
            if not first:
                before = top[h]
                high = jnp.maximum(before[:, :1], high)
            weights = jnp.exp2(scores - high).astype(jnp.bfloat16)
            value = jnp.concatenate([kv[:, NOPE:], ones], axis=1)
            summed = jnp.dot(weights, value, preferred_element_type=jnp.float32)
            if not first:
                summed = summed + acc[h] * jnp.exp2(before[:, :1] - high)
            if last:
                att[h] = (summed[:, :VDIM] / summed[:, VDIM:]).astype(jnp.bfloat16)
            else:
                top[h] = jnp.broadcast_to(high, (ROWS, 128))
                acc[h] = summed

        @pl.loop(0, HEADS // 2)
        def _(i):
            one(i * 2)
            one(i * 2 + 1)

    def landed_slot(slot):
        for made in arrivals[slot]:
            made.wait_recv()

    shared = {0: share(0)}
    for h in range(HEADS):
        loads["up", h].wait()
    shared[0].wait_recv()
    attend(0, True, False)
    landed_slot(1)
    shared[1] = share(1)
    landed_slot(3)
    shared[3] = share(3)
    shared[1].wait_recv()
    attend(1, False, False)
    landed_slot(2)
    shared[2] = share(2)
    shared[3].wait_recv()
    attend(3, False, False)
    shared[2].wait_recv()
    attend(2, False, True)

    above, below, far = turn(z, 1), turn(z, 3), turn(z, 2)
    left, right = pl.ds(0, HALF), pl.ds(HALF, HALF)
    copies = {}

    def copy(src, dst, j, n, to):
        made = remote(src, dst, send.at[j, n], recv.at[j, n], to)
        made.start()
        sent.append(made)
        copies[j, n] = made

    def own_residual(j):
        return residual[:, columns[j]].astype(jnp.float32)

    def spread(j, side):
        copy(part.at[j, side, far, :, left], early.at[j, 0, side], j, 0, z_to[1])
        copy(part.at[j, side, far, :, right], early.at[j, 1, side], j, 1, z_to[3])
        copy(part.at[j, side, above, :, right], late.at[j, 0, side, :, right], j, 2, z_to[1])
        copy(part.at[j, side, below, :, left], late.at[j, 1, side, :, left], j, 3, z_to[3])

    def relay(j, side):
        copies[j, 0].wait_recv()
        mine = part.at[j, side, above, :, left]
        mine[...] = (wide(mine) + wide(early.at[j, 0, side])).astype(jnp.bfloat16)
        copy(mine, late.at[j, 0, side, :, left], j, 4, z_to[1])
        copies[j, 1].wait_recv()
        mine = part.at[j, side, below, :, right]
        mine[...] = (wide(mine) + wide(early.at[j, 1, side])).astype(jnp.bfloat16)
        copy(mine, late.at[j, 1, side, :, right], j, 5, z_to[3])

    def landed(j):
        for n in (2, 3, 4, 5):
            copies[j, n].wait_recv()

    def ring_sum(j, side):
        return wide(part.at[j, side, z]) + wide(late.at[j, 0, side]) + wide(late.at[j, 1, side])

    def finish(j, value):
        final[j] = value.astype(jnp.bfloat16)
        copy(final.at[j], out.at[0, :, columns[j]], j, 7, pp_to)

    def product(j):
        loads["w", j].wait()
        heads = jnp.concatenate([att[h] for h in range(HEADS)], axis=1)
        made = jnp.dot(heads, wv[j], preferred_element_type=jnp.float32)
        part[j] = made.astype(jnp.bfloat16).reshape(2, 4, LATROWS, PIECE)

    def z_step(j, step):
        if step == 0:
            product(j)
            spread(j, slice(None))
        elif step == 1:
            relay(j, slice(None))
        elif step == 2:
            landed(j)
            part[j, a, z] = (ring_sum(j, a) + own_residual(j)).astype(jnp.bfloat16)
            copy(part.at[j, a, z], crossed.at[j, 0], j, 6, x_to)
        elif step == 3:
            copies[j, 6].wait_recv()
            finish(j, ring_sum(j, 1 - a) + wide(crossed.at[j, 0]))

    def x_step(j, step):
        if step == 0:
            product(j)
            part[j, a, z] = (wide(part.at[j, a, z]) + own_residual(j)).astype(jnp.bfloat16)
            copy(part.at[j, a], crossed.at[j], j, 6, x_to)
        elif step == 1:
            copies[j, 6].wait_recv()
            part[j, 1 - a] = (wide(part.at[j, 1 - a]) + wide(crossed.at[j])).astype(jnp.bfloat16)
            spread(j, 1 - a)
        elif step == 2:
            relay(j, 1 - a)
        elif step == 3:
            landed(j)
            finish(j, ring_sum(j, 1 - a))

    steps = {"z": z_step, "x": x_step}
    loads["residual"].wait()
    for j, kind in enumerate(PIECES):
        steps[kind](j, 0)
    for step in range(1, len(PIECES) + 3):
        for j, kind in enumerate(PIECES):
            if 1 <= step - j < 4:
                steps[kind](j, step - j)
    for j in range(len(PIECES)):
        copies[j, 7].wait_recv()
    for made in sent:
        made.wait_send()


def local(queries, latents, latent_gain, w_ukv, w_o, residual, block_order):
    n = len(PIECES)
    hbm = pl.BlockSpec(memory_space=pltpu.HBM)
    bf16, f32 = jnp.bfloat16, jnp.float32
    dma = pltpu.SemaphoreType.DMA
    return pl.pallas_call(
        layer_kernel,
        out_shape=jax.ShapeDtypeStruct((1, LATROWS, D), bf16),
        in_specs=[hbm] * 8,
        out_specs=pl.BlockSpec(memory_space=pltpu.VMEM),
        scratch_shapes=[
            pltpu.VMEM((LATROWS, LATENT + ROPE), bf16),
            pltpu.VMEM((1, LATENT), f32),
            pltpu.VMEM((2, BLOCK + 16, 128), f32),
            pltpu.SMEM((1, 16), jnp.int32),
            pltpu.VMEM((ROWS, HEADS * (NOPE + ROPE)), bf16),
            pltpu.VMEM((HEADS, LATENT, 256), bf16),
            pltpu.VMEM((n, HEADS * VDIM, PIECE), bf16),
            pltpu.VMEM((LATROWS, D), bf16),
            pltpu.VMEM((4, 2, 2, 2, 4, 16, KW), bf16),
            pltpu.VMEM((HEADS, ROWS, 256), bf16),
            pltpu.VMEM((HEADS, ROWS, 128), f32),
            pltpu.VMEM((HEADS, ROWS, 256), f32),
            pltpu.VMEM((HEADS, ROWS, VDIM), bf16),
            pltpu.VMEM((n, 2, 4, LATROWS, PIECE), bf16),
            pltpu.VMEM((n, 2, 2, LATROWS, HALF), bf16),
            pltpu.VMEM((n, 2, 2, LATROWS, PIECE), bf16),
            pltpu.VMEM((n, 4, LATROWS, PIECE), bf16),
            pltpu.VMEM((n, LATROWS, PIECE), bf16),
            dma((6,)),
            dma((HEADS,)),
            dma((n,)),
            dma((17,)),
            dma((17,)),
            dma((n, 8)),
            dma((n, 8)),
        ],
        compiler_params=pltpu.CompilerParams(
            collective_id=0, has_side_effects=True, vmem_limit_bytes=58 * 2**20
        ),
        name="layer",
    )(latents, latent_gain, jnp.asarray(rope_tables()), block_order, queries, w_ukv, w_o, residual)


def solution(mesh):
    in_specs = (
        P("pp", "ctx", "tp"),
        P("pp", ("ctx", "tp"), None),
        P("pp", None),
        P("pp", None, "tp"),
        P("pp", "tp", None),
        P("pp", ("ctx", "tp"), None),
        P("pp", None),
    )
    out_specs = P("pp", ("ctx", "tp"), None)
    return jax.shard_map(local, mesh=mesh, in_specs=in_specs, out_specs=out_specs, check_vma=False)
```

time: 102 us -> 96.2 us (0.943)
  local copies, waits for them, and re-layouts: 7.88 us -> 1.82 us
    unnamed x19 -> x1, local copies, waits for them, and re-layouts: 7.88 us -> 1.82 us
    pallas_call x3 -> x1, Pallas kernels: 93.9 us -> 94.2 us  [local(): pl.pallas_call(layer_kernel, out_shape=jax.ShapeDtypeStruct((1, LATROWS,...]
where the time goes in v2:
time: 96.2 us; the launch traced here: 96 us
  Pallas kernels  94.2 us (98%)
  local copies, waits for them, and re-layouts  1.82 us (2%)
    pallas_call x1, Pallas kernels, local(): pl.pallas_call(layer_kernel, out_shape=jax.ShapeDtypeStruct((1, LATROWS,...  94.2 us

profile of v2, /device:TPU:0, one launch (start us, length us, event | category | flops | bytes accessed | tf_op | source)
XLA Modules:
  0.0 96.0 jit_solution(10056522887939211495)
XLA Ops:
  0.0 94.2 %layer.1 = bf16[1,32,7168]{2,1,0:T(8,128)(2,1)} custom-call(bf16[1,32,576]{2,1,0:T(8,128)(2,1)} %lat_in.1, f32[1,512]{1,0:T(1,128)} %gain_in.1, f32[2,144,128]{2,1,0:T(8,128)} %constant.2.clone.tables_in, s32[1,16]{1,0:T(1,128)} %order_in.1, bf16[1,256,1536]{2,1,0:T(8,128)(2,1)} %q_in.1, bf16[1,512,2048]{2,1,0:T(8,128)(2,1)} %up_in.1, ...), custom_call_target="tpu_custom_call" | custom-call | tf_op jit(solution)/shard_map/layer/pallas_call | solution.py:341
  94.2 1.8 %copy.10 = bf16[1,32,7168]{2,1,0:T(8,128)(2,1)} copy(bf16[1,32,7168]{2,1,0:T(8,128)(2,1)} %layer.1) | data formatting | bytes 917504

commit v3 on v2

--- a/solution.py
+++ b/solution.py
@@ -21,7 +21,11 @@
 CHUNK = 512
 PIECE = 1024
 HALF = PIECE // 2
-PIECES = ("z", "x", "z", "x", "z", "x", "z")
+PIECES = ("x", "z", "x", "z", "x", "z", "z")
+ORDER = (
+    (1, 1), (3, 1), (0, 1), (5, 1), (6, 1), (2, 1), (1, 2), (3, 2), (0, 2), (4, 1), (5, 2),
+    (1, 3), (6, 2), (3, 3), (2, 2), (0, 3), (5, 3), (4, 2), (6, 3), (2, 3), (4, 3),
+)
 SCALE2 = 0.135 * math.log2(math.e)
 
 MESH = pl.DeviceIdType.MESH
@@ -71,8 +75,8 @@
 def layer_kernel(
     lat_in, gain_in, tables_in, order_in, q_in, up_in, w_in, residual_in,
     out,
-    lat, gain, tables, order, q, up, wv, residual,
-    kl, qcat, top, acc, att,
+    lat, gain, tables, order, q, up_k, up_v, wv, residual,
+    kl, q_t, up_vt, key, value_t, bias, top, acc, att,
     part, early, late, crossed, final,
     load_sem, up_sem, w_sem, g_send, g_recv, send, recv,
 ):
@@ -103,7 +107,9 @@
     load("tables", tables_in, tables, load_sem.at[3])
     load("q", q_in.at[0], q, load_sem.at[4])
     for h in range(HEADS):
-        load(("up", h), up_in.at[0, :, pl.ds(h * 256, 256)], up.at[h], up_sem.at[h])
+        at = pl.ds(h * VDIM, VDIM)
+        load(("k", h), up_in.at[0, :, pl.ds(h * 256, NOPE)], up_k.at[:, at], up_sem.at[h])
+        load(("v", h), up_in.at[0, :, pl.ds(h * 256 + NOPE, VDIM)], up_v.at[:, at], up_sem.at[8 + h])
     columns = [pl.ds(j * PIECE, PIECE) for j in range(len(PIECES))]
     for j in range(len(PIECES)):
         load(("w", j), w_in.at[0, :, columns[j]], wv.at[j], w_sem.at[j])
@@ -117,7 +123,7 @@
     normed = (low_rank * scale * gain[...]).astype(jnp.bfloat16)
     twice = jnp.concatenate([rows[:, LATENT:], rows[:, LATENT:]], axis=1)
     cos, sin = rotation(tables, order[0, c * 2 + a], z * LATROWS, LATROWS)
-    roped = (twice * cos + swapped(twice) * sin).astype(jnp.bfloat16)
+    roped = ((twice * cos + swapped(twice) * sin) * SCALE2).astype(jnp.bfloat16)
     own = jnp.concatenate([normed, roped], axis=1)
     kl[0, 0, 0, 0, 0] = own[:16]
     kl[0, 1, 0, 0, 0] = own[16:]
@@ -142,18 +148,20 @@
             both = q[at, pair * 384 : (pair + 1) * 384].astype(jnp.float32)
             v = jnp.concatenate([both[:, 128:192], both[:, 320:384]], axis=1)
             turned = v * cos + swapped(v) * sin
-            low = jnp.where(lane < ROPE, turned, 0.0)
-            high = jnp.where(lane < ROPE, 0.0, turned)
-            qcat[pair * 2, at, :] = jnp.concatenate([both[:, :128], low], axis=1).astype(jnp.bfloat16)
-            qcat[pair * 2 + 1, at, :] = jnp.concatenate([both[:, 192:320], high], axis=1).astype(
-                jnp.bfloat16
-            )
+            q_t[pair * 2, :NOPE, at] = both[:, :128].T.astype(jnp.bfloat16)
+            q_t[pair * 2, NOPE:, at] = jnp.where(lane < ROPE, turned, 0.0).T.astype(jnp.bfloat16)
+            q_t[pair * 2 + 1, :NOPE, at] = both[:, 192:320].T.astype(jnp.bfloat16)
+            q_t[pair * 2 + 1, NOPE:, at] = jnp.where(lane < ROPE, 0.0, turned).T.astype(jnp.bfloat16)
 
     to_x.wait_recv()
     near = []
     for i, n in enumerate((1, 3, 2)):
         near.append(push(kl.at[0, 0, 0, :, 0], kl.at[0, 0, 0, :, 4 - n], 1 + i, z_to[n]))
         near.append(push(kl.at[0, 1, 0, :, 0], kl.at[0, 1, 0, :, 4 - n], 4 + i, y_to[n]))
+    for h in range(HEADS):
+        loads["v", h].wait()
+        at = pl.ds(h * VDIM, VDIM)
+        up_vt[at, :] = up_v[:, at].astype(jnp.float32).T.astype(jnp.bfloat16)
     for made in near:
         made.wait_recv()
     arrivals = {}
@@ -166,83 +174,91 @@
     def share(slot):
         return push(kl.at[slot, :, 0], kl.at[slot, :, 1], 13 + slot, k_to)
 
-    row = lax.broadcasted_iota(jnp.int32, (ROWS, 1), 0)
-    base = jnp.where(row < BLOCK, order[0, c * 2], order[0, c * 2 + 1])
-    query_at = base * BLOCK + lax.rem(row, BLOCK)
-    spot = lax.broadcasted_iota(jnp.int32, (1, 128), 1)
-    minor = lax.rem(spot, 64) // 16
-    deep = lax.rem(spot, 16)
-
-    def key_places(slot):
-        groups = []
-        for core in range(2):
-            there = turn(y, slot) * 2 + (k if core == 0 else 1 - k)
-            block = jnp.where(spot < 64, order[0, there * 2 + a], order[0, there * 2 + 1 - a])
-            groups.append(block * BLOCK + lax.rem(minor + z, 4) * LATROWS + deep)
-        for core in range(2):
-            block = jnp.zeros_like(spot)
-            for m in range(4):
-                there = turn(y, m) * 2 + (k if core == 0 else 1 - k)
-                here = jnp.where(spot < 64, order[0, there * 2 + a], order[0, there * 2 + 1 - a])
-                block = jnp.where(minor == m, here, block)
-            groups.append(block * BLOCK + turn(z, slot) * LATROWS + 16 + deep)
-        return jnp.concatenate(groups, axis=1)
-
-    ones = jnp.ones((CHUNK, VDIM), jnp.bfloat16)
-
-    def attend(slot, first, last):
-        allowed = key_places(slot) <= query_at
-
-        def one(h):
-            latent = kl[slot].reshape(CHUNK, KW)
-            kv = jnp.dot(latent[:, :LATENT], up[h], preferred_element_type=jnp.float32)
-            kv = kv.astype(jnp.bfloat16)
-            key = jnp.concatenate([kv[:, :NOPE], latent[:, LATENT:]], axis=1)
-            scores = lax.dot_general(
-                qcat[h], key, (((1,), (1,)), ((), ())), preferred_element_type=jnp.float32
-            )
-            scores = jnp.where(allowed, scores * SCALE2, -1e30)
-            high = jnp.max(scores, axis=-1, keepdims=True)
+    row = lax.broadcasted_iota(jnp.int32, (BLOCK, BLOCK), 0)
+    second = row >= 64
+    minor = lax.rem(row, 64) // 16
+    deep = lax.rem(row, 16)
+    query_in = lax.broadcasted_iota(jnp.int32, (BLOCK, BLOCK), 1)
+    query_at = [order[0, c * 2 + n] * BLOCK + query_in for n in range(2)]
+
+    def mask(slot):
+        for half in range(2):
+            for core in range(2):
+                here = k if core == 0 else 1 - k
+                if half == 0:
+                    there = (turn(y, slot) * 2 + here) * 2
+                    block = jnp.where(second, order[0, there + 1 - a], order[0, there + a])
+                    key_at = block * BLOCK + lax.rem(minor + z, 4) * LATROWS + deep
+                else:
+                    block = jnp.zeros_like(row)
+                    for m in range(4):
+                        there = (turn(y, m) * 2 + here) * 2
+                        one = jnp.where(second, order[0, there + 1 - a], order[0, there + a])
+                        block = jnp.where(minor == m, one, block)
+                    key_at = block * BLOCK + turn(z, slot) * LATROWS + 16 + deep
+                for n in range(2):
+                    bias[pl.ds((half * 2 + core) * BLOCK, BLOCK), pl.ds(n * BLOCK, BLOCK)] = jnp.where(
+                        key_at <= query_at[n], 0.0, -1e30
+                    )
+
+    ones = jnp.ones((16, CHUNK), jnp.bfloat16)
+
+    def attend(slot, first, last, between):
+        mask(slot)
+        latent = kl[slot].reshape(CHUNK, KW)
+        low_rank, key_rope = latent[:, :LATENT], latent[:, LATENT:]
+        for n in range(4):
+            at = pl.ds(n * 256, 256)
+            made = jnp.dot(low_rank, up_k[:, at], preferred_element_type=jnp.float32)
+            key[:, at] = (made * SCALE2).astype(jnp.bfloat16)
+        for n in range(4):
+            at = pl.ds(n * 256, 256)
+            value_t[at, :] = lax.dot_general(
+                up_vt[at, :], low_rank, (((1,), (1,)), ((), ())), preferred_element_type=jnp.float32
+            ).astype(jnp.bfloat16)
+        for h in range(HEADS):
+            if h == 5:
+                between()
+            at = pl.ds(h * VDIM, VDIM)
+            keys = jnp.concatenate([key[:, at], key_rope], axis=1)
+            scores = jnp.dot(keys, q_t[h], preferred_element_type=jnp.float32) + bias[...]
+            high = jnp.max(scores, axis=0, keepdims=True)
             if not first:
-                before = top[h]
-                high = jnp.maximum(before[:, :1], high)
+                before = top[h, :1]
+                high = jnp.maximum(before, high)
             weights = jnp.exp2(scores - high).astype(jnp.bfloat16)
-            value = jnp.concatenate([kv[:, NOPE:], ones], axis=1)
-            summed = jnp.dot(weights, value, preferred_element_type=jnp.float32)
+            values = jnp.concatenate([value_t[at, :], ones], axis=0)
+            summed = jnp.dot(values, weights, preferred_element_type=jnp.float32)
             if not first:
-                summed = summed + acc[h] * jnp.exp2(before[:, :1] - high)
+                summed = summed + acc[h] * jnp.exp2(before - high)
             if last:
-                att[h] = (summed[:, :VDIM] / summed[:, VDIM:]).astype(jnp.bfloat16)
+                shared_out = summed[:VDIM] / summed[VDIM : VDIM + 1]
+                att[:, at] = shared_out.T.astype(jnp.bfloat16)
             else:
-                top[h] = jnp.broadcast_to(high, (ROWS, 128))
+                top[h] = jnp.broadcast_to(high, (8, ROWS))
                 acc[h] = summed
-
-        @pl.loop(0, HEADS // 2)
-        def _(i):
-            one(i * 2)
-            one(i * 2 + 1)
 
     def landed_slot(slot):
         for made in arrivals[slot]:
             made.wait_recv()
 
     shared = {0: share(0)}
+
+    def pass_on(*slots):
+        for slot in slots:
+            landed_slot(slot)
+            shared[slot] = share(slot)
+
     for h in range(HEADS):
-        loads["up", h].wait()
+        loads["k", h].wait()
     shared[0].wait_recv()
-    attend(0, True, False)
-    landed_slot(1)
-    shared[1] = share(1)
-    landed_slot(3)
-    shared[3] = share(3)
+    attend(0, True, False, lambda: pass_on(1, 3))
     shared[1].wait_recv()
-    attend(1, False, False)
-    landed_slot(2)
-    shared[2] = share(2)
+    attend(1, False, False, lambda: pass_on(2))
     shared[3].wait_recv()
-    attend(3, False, False)
+    attend(3, False, False, lambda: None)
     shared[2].wait_recv()
-    attend(2, False, True)
+    attend(2, False, True, lambda: None)
 
     above, below, far = turn(z, 1), turn(z, 3), turn(z, 2)
     left, right = pl.ds(0, HALF), pl.ds(HALF, HALF)
@@ -286,8 +302,7 @@
 
     def product(j):
         loads["w", j].wait()
-        heads = jnp.concatenate([att[h] for h in range(HEADS)], axis=1)
-        made = jnp.dot(heads, wv[j], preferred_element_type=jnp.float32)
+        made = jnp.dot(att[...], wv[j], preferred_element_type=jnp.float32)
         part[j] = made.astype(jnp.bfloat16).reshape(2, 4, LATROWS, PIECE)
 
     def z_step(j, step):
@@ -323,10 +338,8 @@
     loads["residual"].wait()
     for j, kind in enumerate(PIECES):
         steps[kind](j, 0)
-    for step in range(1, len(PIECES) + 3):
-        for j, kind in enumerate(PIECES):
-            if 1 <= step - j < 4:
-                steps[kind](j, step - j)
+    for j, step in ORDER:
+        steps[PIECES[j]](j, step)
     for j in range(len(PIECES)):
         copies[j, 7].wait_recv()
     for made in sent:
@@ -349,21 +362,26 @@
             pltpu.VMEM((2, BLOCK + 16, 128), f32),
             pltpu.SMEM((1, 16), jnp.int32),
             pltpu.VMEM((ROWS, HEADS * (NOPE + ROPE)), bf16),
-            pltpu.VMEM((HEADS, LATENT, 256), bf16),
+            pltpu.VMEM((LATENT, HEADS * NOPE), bf16),
+            pltpu.VMEM((LATENT, HEADS * VDIM), bf16),
             pltpu.VMEM((n, HEADS * VDIM, PIECE), bf16),
             pltpu.VMEM((LATROWS, D), bf16),
             pltpu.VMEM((4, 2, 2, 2, 4, 16, KW), bf16),
-            pltpu.VMEM((HEADS, ROWS, 256), bf16),
-            pltpu.VMEM((HEADS, ROWS, 128), f32),
-            pltpu.VMEM((HEADS, ROWS, 256), f32),
-            pltpu.VMEM((HEADS, ROWS, VDIM), bf16),
+            pltpu.VMEM((HEADS, 256, ROWS), bf16),
+            pltpu.VMEM((HEADS * VDIM, LATENT), bf16),
+            pltpu.VMEM((CHUNK, HEADS * NOPE), bf16),
+            pltpu.VMEM((HEADS * VDIM, CHUNK), bf16),
+            pltpu.VMEM((CHUNK, ROWS), f32),
+            pltpu.VMEM((HEADS, 8, ROWS), f32),
+            pltpu.VMEM((HEADS, VDIM + 16, ROWS), f32),
+            pltpu.VMEM((ROWS, HEADS * VDIM), bf16),
             pltpu.VMEM((n, 2, 4, LATROWS, PIECE), bf16),
             pltpu.VMEM((n, 2, 2, LATROWS, HALF), bf16),
             pltpu.VMEM((n, 2, 2, LATROWS, PIECE), bf16),
             pltpu.VMEM((n, 4, LATROWS, PIECE), bf16),
             pltpu.VMEM((n, LATROWS, PIECE), bf16),
             dma((6,)),
-            dma((HEADS,)),
+            dma((2 * HEADS,)),
             dma((n,)),
             dma((17,)),
             dma((17,)),

time: 96.2 us -> 76.3 us (0.79)
  Pallas kernels: 94.2 us -> 74.4 us
    pallas_call x1, Pallas kernels: 94.2 us -> 74.4 us  [local(): pl.pallas_call(layer_kernel, out_shape=jax.ShapeDtypeStruct((1, LATROWS,...]
where the time goes in v3:
time: 76.3 us; the launch traced here: 76.2 us
  Pallas kernels  74.4 us (98%)
  local copies, waits for them, and re-layouts  1.82 us (2%)
    pallas_call x1, Pallas kernels, local(): pl.pallas_call(layer_kernel, out_shape=jax.ShapeDtypeStruct((1, LATROWS,...  74.4 us
    unnamed x1, local copies, waits for them, and re-layouts  1.82 us

profile of v3, /device:TPU:0, one launch (start us, length us, event | category | flops | bytes accessed | tf_op | source)
XLA Modules:
  0.0 76.2 jit_solution(6507460929588590308)
XLA Ops:
  0.0 74.4 %layer.1 = bf16[1,32,7168]{2,1,0:T(8,128)(2,1)} custom-call(bf16[1,32,576]{2,1,0:T(8,128)(2,1)} %lat_in.1, f32[1,512]{1,0:T(1,128)} %gain_in.1, f32[2,144,128]{2,1,0:T(8,128)} %constant.2.clone.tables_in, s32[1,16]{1,0:T(1,128)} %order_in.1, bf16[1,256,1536]{2,1,0:T(8,128)(2,1)} %q_in.1, bf16[1,512,2048]{2,1,0:T(8,128)(2,1)} %up_in.1, ...), custom_call_target="tpu_custom_call" | custom-call | tf_op jit(solution)/shard_map/layer/pallas_call | solution.py:354
  74.4 1.8 %copy.10 = bf16[1,32,7168]{2,1,0:T(8,128)(2,1)} copy(bf16[1,32,7168]{2,1,0:T(8,128)(2,1)} %layer.1) | data formatting | bytes 917504

commit v4 on v3

--- a/solution.py
+++ b/solution.py
@@ -90,10 +90,6 @@
     k_to = device(y, 1 - k, a, z, p)
     pp_to = device(y, k, 1 - a, z, 1 - p)
 
-    barrier = pltpu.get_barrier_semaphore()
-    for to in [*z_to.values(), *y_to.values(), x_to, k_to, pp_to]:
-        pl.semaphore_signal(barrier, inc=1, device_id=to, device_id_type=MESH)
-
     loads = {}
 
     def load(name, src, dst, sem):
@@ -105,15 +101,16 @@
     load("order", order_in, order, load_sem.at[1])
     load("gain", gain_in, gain, load_sem.at[2])
     load("tables", tables_in, tables, load_sem.at[3])
+    barrier = pltpu.get_barrier_semaphore()
+    for to in [*z_to.values(), *y_to.values(), x_to, k_to, pp_to]:
+        pl.semaphore_signal(barrier, inc=1, device_id=to, device_id_type=MESH)
+
     load("q", q_in.at[0], q, load_sem.at[4])
     for h in range(HEADS):
         at = pl.ds(h * VDIM, VDIM)
         load(("k", h), up_in.at[0, :, pl.ds(h * 256, NOPE)], up_k.at[:, at], up_sem.at[h])
         load(("v", h), up_in.at[0, :, pl.ds(h * 256 + NOPE, VDIM)], up_v.at[:, at], up_sem.at[8 + h])
     columns = [pl.ds(j * PIECE, PIECE) for j in range(len(PIECES))]
-    for j in range(len(PIECES)):
-        load(("w", j), w_in.at[0, :, columns[j]], wv.at[j], w_sem.at[j])
-    load("residual", residual_in.at[0], residual, load_sem.at[5])
 
     for name in ("lat", "order", "gain", "tables"):
         loads[name].wait()
@@ -165,10 +162,17 @@
     for made in near:
         made.wait_recv()
     arrivals = {}
-    for i, n in enumerate((3, 1, 2)):
+    for i, n in enumerate((3, 1)):
         arrivals[4 - n] = (
             push(kl.at[0, 0, 0], kl.at[4 - n, 0, 0], 7 + i, y_to[n]),
-            push(kl.at[0, 1, 0], kl.at[4 - n, 1, 0], 10 + i, z_to[n]),
+            push(kl.at[0, 1, 0], kl.at[4 - n, 1, 0], 9 + i, z_to[n]),
+        )
+
+    def forward(slot):
+        side, to = (0, 3) if slot == 1 else (1, 1)
+        return (
+            push(kl.at[slot, 0, 0, side], kl.at[2, 0, 0, side], 11 + side, y_to[to]),
+            push(kl.at[slot, 1, 0, side], kl.at[2, 1, 0, side], 17 + side, z_to[to]),
         )
 
     def share(slot):
@@ -245,13 +249,22 @@
     shared = {0: share(0)}
 
     def pass_on(*slots):
+        if slots == (1, 3):
+            landed_slot(1)
+            ahead = forward(1)
+            landed_slot(3)
+            arrivals[2] = ahead + forward(3)
+        else:
+            landed_slot(2)
         for slot in slots:
-            landed_slot(slot)
             shared[slot] = share(slot)
 
     for h in range(HEADS):
         loads["k", h].wait()
     shared[0].wait_recv()
+    load("residual", residual_in.at[0], residual, load_sem.at[5])
+    for j in range(len(PIECES)):
+        load(("w", j), w_in.at[0, :, columns[j]], wv.at[j], w_sem.at[j])
     attend(0, True, False, lambda: pass_on(1, 3))
     shared[1].wait_recv()
     attend(1, False, False, lambda: pass_on(2))
@@ -383,8 +396,8 @@
             dma((6,)),
             dma((2 * HEADS,)),
             dma((n,)),
-            dma((17,)),
-            dma((17,)),
+            dma((19,)),
+            dma((19,)),
             dma((n, 8)),
             dma((n, 8)),
         ],

time: 76.3 us -> 72.1 us (0.945)
  Pallas kernels: 74.4 us -> 70.1 us
    pallas_call x1, Pallas kernels: 74.4 us -> 70.1 us  [local(): pl.pallas_call(layer_kernel, out_shape=jax.ShapeDtypeStruct((1, LATROWS,...]
where the time goes in v4:
time: 72.1 us; the launch traced here: 71.9 us
  Pallas kernels  70.1 us (97%)
  local copies, waits for them, and re-layouts  1.82 us (3%)
    pallas_call x1, Pallas kernels, local(): pl.pallas_call(layer_kernel, out_shape=jax.ShapeDtypeStruct((1, LATROWS,...  70.1 us
    unnamed x1, local copies, waits for them, and re-layouts  1.82 us

profile of v4, /device:TPU:0, one launch (start us, length us, event | category | flops | bytes accessed | tf_op | source)
XLA Modules:
  0.0 71.9 jit_solution(1690075868002646172)
XLA Ops:
  0.0 70.1 %layer.1 = bf16[1,32,7168]{2,1,0:T(8,128)(2,1)} custom-call(bf16[1,32,576]{2,1,0:T(8,128)(2,1)} %lat_in.1, f32[1,512]{1,0:T(1,128)} %gain_in.1, f32[2,144,128]{2,1,0:T(8,128)} %constant.2.clone.tables_in, s32[1,16]{1,0:T(1,128)} %order_in.1, bf16[1,256,1536]{2,1,0:T(8,128)(2,1)} %q_in.1, bf16[1,512,2048]{2,1,0:T(8,128)(2,1)} %up_in.1, ...), custom_call_target="tpu_custom_call" | custom-call | tf_op jit(solution)/shard_map/layer/pallas_call | solution.py:367
  70.1 1.8 %copy.10 = bf16[1,32,7168]{2,1,0:T(8,128)(2,1)} copy(bf16[1,32,7168]{2,1,0:T(8,128)(2,1)} %layer.1) | data formatting | bytes 917504

commit v5 on v4

--- a/solution.py
+++ b/solution.py
@@ -208,39 +208,64 @@
     ones = jnp.ones((16, CHUNK), jnp.bfloat16)
 
     def attend(slot, first, last, between):
-        mask(slot)
         latent = kl[slot].reshape(CHUNK, KW)
         low_rank, key_rope = latent[:, :LATENT], latent[:, LATENT:]
-        for n in range(4):
+
+        def make_keys(n):
             at = pl.ds(n * 256, 256)
             made = jnp.dot(low_rank, up_k[:, at], preferred_element_type=jnp.float32)
             key[:, at] = (made * SCALE2).astype(jnp.bfloat16)
-        for n in range(4):
+
+        def make_values(n):
             at = pl.ds(n * 256, 256)
             value_t[at, :] = lax.dot_general(
                 up_vt[at, :], low_rank, (((1,), (1,)), ((), ())), preferred_element_type=jnp.float32
             ).astype(jnp.bfloat16)
+
+        def score(h):
+            keys = jnp.concatenate([key[:, pl.ds(h * VDIM, VDIM)], key_rope], axis=1)
+            return jnp.dot(keys, q_t[h], preferred_element_type=jnp.float32) + bias[...]
+
+        def soften(h, scores):
+            high = jnp.max(scores, axis=0, keepdims=True)
+            shrink = None
+            if not first:
+                before = top[h, :1]
+                high = jnp.maximum(before, high)
+                shrink = jnp.exp2(before - high)
+            if not last:
+                top[h] = jnp.broadcast_to(high, (8, ROWS))
+            return jnp.exp2(scores - high).astype(jnp.bfloat16), shrink
+
+        def gather_values(h, weights, shrink):
+            at = pl.ds(h * VDIM, VDIM)
+            values = jnp.concatenate([value_t[at, :], ones], axis=0)
+            summed = jnp.dot(values, weights, preferred_element_type=jnp.float32)
+            if not first:
+                summed = summed + acc[h] * shrink
+            if last:
+                att[:, at] = (summed[:VDIM] / summed[VDIM : VDIM + 1]).T.astype(jnp.bfloat16)
+            else:
+                acc[h] = summed
+
+        make_keys(0)
+        mask(slot)
+        make_values(0)
+        scores, waiting = score(0), None
         for h in range(HEADS):
             if h == 5:
                 between()
-            at = pl.ds(h * VDIM, VDIM)
-            keys = jnp.concatenate([key[:, at], key_rope], axis=1)
-            scores = jnp.dot(keys, q_t[h], preferred_element_type=jnp.float32) + bias[...]
-            high = jnp.max(scores, axis=0, keepdims=True)
-            if not first:
-                before = top[h, :1]
-                high = jnp.maximum(before, high)
-            weights = jnp.exp2(scores - high).astype(jnp.bfloat16)
-            values = jnp.concatenate([value_t[at, :], ones], axis=0)
-            summed = jnp.dot(values, weights, preferred_element_type=jnp.float32)
-            if not first:
-                summed = summed + acc[h] * jnp.exp2(before - high)
-            if last:
-                shared_out = summed[:VDIM] / summed[VDIM : VDIM + 1]
-                att[:, at] = shared_out.T.astype(jnp.bfloat16)
-            else:
-                top[h] = jnp.broadcast_to(high, (8, ROWS))
-                acc[h] = summed
+            more = h % 2 == 0 and h < 6
+            if more:
+                make_keys(h // 2 + 1)
+            following = score(h + 1) if h < HEADS - 1 else None
+            weights, shrink = soften(h, scores)
+            if more:
+                make_values(h // 2 + 1)
+            if waiting:
+                gather_values(*waiting)
+            waiting, scores = (h, weights, shrink), following
+        gather_values(*waiting)
 
     def landed_slot(slot):
         for made in arrivals[slot]:

time: 72.1 us -> 66.5 us (0.922)
  Pallas kernels: 70.1 us -> 64.5 us
    pallas_call x1, Pallas kernels: 70.1 us -> 64.5 us  [local(): pl.pallas_call(layer_kernel, out_shape=jax.ShapeDtypeStruct((1, LATROWS,...]
where the time goes in v5:
time: 66.5 us; the launch traced here: 66.3 us
  Pallas kernels  64.5 us (97%)
  local copies, waits for them, and re-layouts  1.82 us (3%)
    pallas_call x1, Pallas kernels, local(): pl.pallas_call(layer_kernel, out_shape=jax.ShapeDtypeStruct((1, LATROWS,...  64.5 us
    unnamed x1, local copies, waits for them, and re-layouts  1.82 us

profile of v5, /device:TPU:0, one launch (start us, length us, event | category | flops | bytes accessed | tf_op | source)
XLA Modules:
  0.0 66.3 jit_solution(12263773470749688877)
XLA Ops:
  0.0 64.5 %layer.1 = bf16[1,32,7168]{2,1,0:T(8,128)(2,1)} custom-call(bf16[1,32,576]{2,1,0:T(8,128)(2,1)} %lat_in.1, f32[1,512]{1,0:T(1,128)} %gain_in.1, f32[2,144,128]{2,1,0:T(8,128)} %constant.2.clone.tables_in, s32[1,16]{1,0:T(1,128)} %order_in.1, bf16[1,256,1536]{2,1,0:T(8,128)(2,1)} %q_in.1, bf16[1,512,2048]{2,1,0:T(8,128)(2,1)} %up_in.1, ...), custom_call_target="tpu_custom_call" | custom-call | tf_op jit(solution)/shard_map/layer/pallas_call | solution.py:392
  64.5 1.8 %copy.10 = bf16[1,32,7168]{2,1,0:T(8,128)(2,1)} copy(bf16[1,32,7168]{2,1,0:T(8,128)(2,1)} %layer.1) | data formatting | bytes 917504

commit v6 on v5

--- a/solution.py
+++ b/solution.py
@@ -207,7 +207,7 @@
 
     ones = jnp.ones((16, CHUNK), jnp.bfloat16)
 
-    def attend(slot, first, last, between):
+    def attend(slot, first, last, between, when):
         latent = kl[slot].reshape(CHUNK, KW)
         low_rank, key_rope = latent[:, :LATENT], latent[:, LATENT:]
 
@@ -253,7 +253,7 @@
         make_values(0)
         scores, waiting = score(0), None
         for h in range(HEADS):
-            if h == 5:
+            if h == when:
                 between()
             more = h % 2 == 0 and h < 6
             if more:
@@ -290,13 +290,13 @@
     load("residual", residual_in.at[0], residual, load_sem.at[5])
     for j in range(len(PIECES)):
         load(("w", j), w_in.at[0, :, columns[j]], wv.at[j], w_sem.at[j])
-    attend(0, True, False, lambda: pass_on(1, 3))
+    attend(0, True, False, lambda: pass_on(1, 3), 5)
     shared[1].wait_recv()
-    attend(1, False, False, lambda: pass_on(2))
+    attend(1, False, False, lambda: pass_on(2), 7)
     shared[3].wait_recv()
-    attend(3, False, False, lambda: None)
+    attend(3, False, False, lambda: None, 5)
     shared[2].wait_recv()
-    attend(2, False, True, lambda: None)
+    attend(2, False, True, lambda: None, 5)
 
     above, below, far = turn(z, 1), turn(z, 3), turn(z, 2)
     left, right = pl.ds(0, HALF), pl.ds(HALF, HALF)

time: 66.5 us -> 66.1 us (level)
  no operation moved by 1% of the time
where the time goes in v6:
time: 66.1 us; the launch traced here: 65.9 us
  Pallas kernels  64.1 us (97%)
  local copies, waits for them, and re-layouts  1.82 us (3%)
    pallas_call x1, Pallas kernels, local(): pl.pallas_call(layer_kernel, out_shape=jax.ShapeDtypeStruct((1, LATROWS,...  64.1 us
    unnamed x1, local copies, waits for them, and re-layouts  1.82 us

profile of v6, /device:TPU:0, one launch (start us, length us, event | category | flops | bytes accessed | tf_op | source)
XLA Modules:
  0.0 65.9 jit_solution(374197782229970980)
XLA Ops:
  0.0 64.1 %layer.1 = bf16[1,32,7168]{2,1,0:T(8,128)(2,1)} custom-call(bf16[1,32,576]{2,1,0:T(8,128)(2,1)} %lat_in.1, f32[1,512]{1,0:T(1,128)} %gain_in.1, f32[2,144,128]{2,1,0:T(8,128)} %constant.2.clone.tables_in, s32[1,16]{1,0:T(1,128)} %order_in.1, bf16[1,256,1536]{2,1,0:T(8,128)(2,1)} %q_in.1, bf16[1,512,2048]{2,1,0:T(8,128)(2,1)} %up_in.1, ...), custom_call_target="tpu_custom_call" | custom-call | tf_op jit(solution)/shard_map/layer/pallas_call | solution.py:392
  64.1 1.8 %copy.10 = bf16[1,32,7168]{2,1,0:T(8,128)(2,1)} copy(bf16[1,32,7168]{2,1,0:T(8,128)(2,1)} %layer.1) | data formatting | bytes 917504

commit v7 on v6

--- a/solution.py
+++ b/solution.py
@@ -19,13 +19,13 @@
 D = 7168
 KW = LATENT + 128
 CHUNK = 512
-PIECE = 1024
-HALF = PIECE // 2
-PIECES = ("x", "z", "x", "z", "x", "z", "z")
+PIECES = (("x", 512), ("z", 512), ("z", 512), ("z", 512), ("x", 512), ("z", 512), ("z", 1024), ("z", 1024), ("x", 1024), ("x", 1024))
 ORDER = (
-    (1, 1), (3, 1), (0, 1), (5, 1), (6, 1), (2, 1), (1, 2), (3, 2), (0, 2), (4, 1), (5, 2),
-    (1, 3), (6, 2), (3, 3), (2, 2), (0, 3), (5, 3), (4, 2), (6, 3), (2, 3), (4, 3),
+    (1, 1), (2, 1), (0, 1), (3, 1), (5, 1), (4, 1), (6, 1), (7, 1), (8, 1), (1, 2),
+    (2, 2), (0, 2), (3, 2), (5, 2), (4, 2), (9, 1), (6, 2), (1, 3), (2, 3), (7, 2),
+    (3, 3), (8, 2), (5, 3), (0, 3), (4, 3), (6, 3), (9, 2), (7, 3), (8, 3), (9, 3),
 )
+WIDEST = max(width for _, width in PIECES)
 SCALE2 = 0.135 * math.log2(math.e)
 
 MESH = pl.DeviceIdType.MESH
@@ -110,7 +110,11 @@
         at = pl.ds(h * VDIM, VDIM)
         load(("k", h), up_in.at[0, :, pl.ds(h * 256, NOPE)], up_k.at[:, at], up_sem.at[h])
         load(("v", h), up_in.at[0, :, pl.ds(h * 256 + NOPE, VDIM)], up_v.at[:, at], up_sem.at[8 + h])
-    columns = [pl.ds(j * PIECE, PIECE) for j in range(len(PIECES))]
+    widths = [width for _, width in PIECES]
+    columns = [pl.ds(sum(widths[:j]), widths[j]) for j in range(len(PIECES))]
+    full = [pl.ds(0, width) for width in widths]
+    left = [pl.ds(0, width // 2) for width in widths]
+    right = [pl.ds(width // 2, width // 2) for width in widths]
 
     for name in ("lat", "order", "gain", "tables"):
         loads[name].wait()
@@ -289,7 +293,7 @@
     shared[0].wait_recv()
     load("residual", residual_in.at[0], residual, load_sem.at[5])
     for j in range(len(PIECES)):
-        load(("w", j), w_in.at[0, :, columns[j]], wv.at[j], w_sem.at[j])
+        load(("w", j), w_in.at[0, :, columns[j]], wv.at[:, columns[j]], w_sem.at[j])
     attend(0, True, False, lambda: pass_on(1, 3), 5)
     shared[1].wait_recv()
     attend(1, False, False, lambda: pass_on(2), 7)
@@ -299,7 +303,6 @@
     attend(2, False, True, lambda: None, 5)
 
     above, below, far = turn(z, 1), turn(z, 3), turn(z, 2)
-    left, right = pl.ds(0, HALF), pl.ds(HALF, HALF)
     copies = {}
 
     def copy(src, dst, j, n, to):
@@ -312,38 +315,41 @@
         return residual[:, columns[j]].astype(jnp.float32)
 
     def spread(j, side):
-        copy(part.at[j, side, far, :, left], early.at[j, 0, side], j, 0, z_to[1])
-        copy(part.at[j, side, far, :, right], early.at[j, 1, side], j, 1, z_to[3])
-        copy(part.at[j, side, above, :, right], late.at[j, 0, side, :, right], j, 2, z_to[1])
-        copy(part.at[j, side, below, :, left], late.at[j, 1, side, :, left], j, 3, z_to[3])
+        copy(part.at[j, side, far, :, left[j]], early.at[j, 0, side, :, left[j]], j, 0, z_to[1])
+        copy(part.at[j, side, far, :, right[j]], early.at[j, 1, side, :, left[j]], j, 1, z_to[3])
+        copy(part.at[j, side, above, :, right[j]], late.at[j, 0, side, :, right[j]], j, 2, z_to[1])
+        copy(part.at[j, side, below, :, left[j]], late.at[j, 1, side, :, left[j]], j, 3, z_to[3])
 
     def relay(j, side):
         copies[j, 0].wait_recv()
-        mine = part.at[j, side, above, :, left]
-        mine[...] = (wide(mine) + wide(early.at[j, 0, side])).astype(jnp.bfloat16)
-        copy(mine, late.at[j, 0, side, :, left], j, 4, z_to[1])
+        mine = part.at[j, side, above, :, left[j]]
+        mine[...] = (wide(mine) + wide(early.at[j, 0, side, :, left[j]])).astype(jnp.bfloat16)
+        copy(mine, late.at[j, 0, side, :, left[j]], j, 4, z_to[1])
         copies[j, 1].wait_recv()
-        mine = part.at[j, side, below, :, right]
-        mine[...] = (wide(mine) + wide(early.at[j, 1, side])).astype(jnp.bfloat16)
-        copy(mine, late.at[j, 1, side, :, right], j, 5, z_to[3])
+        mine = part.at[j, side, below, :, right[j]]
+        mine[...] = (wide(mine) + wide(early.at[j, 1, side, :, left[j]])).astype(jnp.bfloat16)
+        copy(mine, late.at[j, 1, side, :, right[j]], j, 5, z_to[3])
 
     def landed(j):
         for n in (2, 3, 4, 5):
             copies[j, n].wait_recv()
 
     def ring_sum(j, side):
-        return wide(part.at[j, side, z]) + wide(late.at[j, 0, side]) + wide(late.at[j, 1, side])
+        here = wide(part.at[j, side, z, :, full[j]])
+        return here + wide(late.at[j, 0, side, :, full[j]]) + wide(late.at[j, 1, side, :, full[j]])
 
     def finish(j, value):
-        final[j] = value.astype(jnp.bfloat16)
-        copy(final.at[j], out.at[0, :, columns[j]], j, 7, pp_to)
+        final[j, :, full[j]] = value.astype(jnp.bfloat16)
+        copy(final.at[j, :, full[j]], out.at[0, :, columns[j]], j, 7, pp_to)
 
     def product(j):
         loads["w", j].wait()
-        made = jnp.dot(att[...], wv[j], preferred_element_type=jnp.float32)
-        part[j] = made.astype(jnp.bfloat16).reshape(2, 4, LATROWS, PIECE)
+        made = jnp.dot(att[...], wv[:, columns[j]], preferred_element_type=jnp.float32)
+        part[j, :, :, :, full[j]] = made.astype(jnp.bfloat16).reshape(2, 4, LATROWS, widths[j])
 
     def z_step(j, step):
+        mine = part.at[j, a, z, :, full[j]]
+        crossing = crossed.at[j, 0, :, full[j]]
         if step == 0:
             product(j)
             spread(j, slice(None))
@@ -351,20 +357,23 @@
             relay(j, slice(None))
         elif step == 2:
             landed(j)
-            part[j, a, z] = (ring_sum(j, a) + own_residual(j)).astype(jnp.bfloat16)
-            copy(part.at[j, a, z], crossed.at[j, 0], j, 6, x_to)
+            mine[...] = (ring_sum(j, a) + own_residual(j)).astype(jnp.bfloat16)
+            copy(mine, crossing, j, 6, x_to)
         elif step == 3:
             copies[j, 6].wait_recv()
-            finish(j, ring_sum(j, 1 - a) + wide(crossed.at[j, 0]))
+            finish(j, ring_sum(j, 1 - a) + wide(crossing))
 
     def x_step(j, step):
+        mine = part.at[j, a, z, :, full[j]]
+        kept = part.at[j, 1 - a, :, :, full[j]]
+        crossing = crossed.at[j, :, :, full[j]]
         if step == 0:
             product(j)
-            part[j, a, z] = (wide(part.at[j, a, z]) + own_residual(j)).astype(jnp.bfloat16)
-            copy(part.at[j, a], crossed.at[j], j, 6, x_to)
+            mine[...] = (wide(mine) + own_residual(j)).astype(jnp.bfloat16)
+            copy(part.at[j, a, :, :, full[j]], crossing, j, 6, x_to)
         elif step == 1:
             copies[j, 6].wait_recv()
-            part[j, 1 - a] = (wide(part.at[j, 1 - a]) + wide(crossed.at[j])).astype(jnp.bfloat16)
+            kept[...] = (wide(kept) + wide(crossing)).astype(jnp.bfloat16)
             spread(j, 1 - a)
         elif step == 2:
             relay(j, 1 - a)
@@ -374,10 +383,10 @@
 
     steps = {"z": z_step, "x": x_step}
     loads["residual"].wait()
-    for j, kind in enumerate(PIECES):
+    for j, (kind, _) in enumerate(PIECES):
         steps[kind](j, 0)
     for j, step in ORDER:
-        steps[PIECES[j]](j, step)
+        steps[PIECES[j][0]](j, step)
     for j in range(len(PIECES)):
         copies[j, 7].wait_recv()
     for made in sent:
@@ -402,7 +411,7 @@
             pltpu.VMEM((ROWS, HEADS * (NOPE + ROPE)), bf16),
             pltpu.VMEM((LATENT, HEADS * NOPE), bf16),
             pltpu.VMEM((LATENT, HEADS * VDIM), bf16),
-            pltpu.VMEM((n, HEADS * VDIM, PIECE), bf16),
+            pltpu.VMEM((HEADS * VDIM, D), bf16),
             pltpu.VMEM((LATROWS, D), bf16),
             pltpu.VMEM((4, 2, 2, 2, 4, 16, KW), bf16),
             pltpu.VMEM((HEADS, 256, ROWS), bf16),
@@ -413,11 +422,11 @@
             pltpu.VMEM((HEADS, 8, ROWS), f32),
             pltpu.VMEM((HEADS, VDIM + 16, ROWS), f32),
             pltpu.VMEM((ROWS, HEADS * VDIM), bf16),
-            pltpu.VMEM((n, 2, 4, LATROWS, PIECE), bf16),
-            pltpu.VMEM((n, 2, 2, LATROWS, HALF), bf16),
-            pltpu.VMEM((n, 2, 2, LATROWS, PIECE), bf16),
-            pltpu.VMEM((n, 4, LATROWS, PIECE), bf16),
-            pltpu.VMEM((n, LATROWS, PIECE), bf16),
+            pltpu.VMEM((n, 2, 4, LATROWS, WIDEST), bf16),
+            pltpu.VMEM((n, 2, 2, LATROWS, WIDEST // 2), bf16),
+            pltpu.VMEM((n, 2, 2, LATROWS, WIDEST), bf16),
+            pltpu.VMEM((n, 4, LATROWS, WIDEST), bf16),
+            pltpu.VMEM((n, LATROWS, WIDEST), bf16),
             dma((6,)),
             dma((2 * HEADS,)),
             dma((n,)),

time: 66.1 us -> 65.8 us (level)
  no operation moved by 1% of the time
where the time goes in v7:
time: 65.8 us; the launch traced here: 65.7 us
  Pallas kernels  63.8 us (97%)
  local copies, waits for them, and re-layouts  1.82 us (3%)
    pallas_call x1, Pallas kernels, local(): pl.pallas_call(layer_kernel, out_shape=jax.ShapeDtypeStruct((1, LATROWS,...  63.8 us
    unnamed x1, local copies, waits for them, and re-layouts  1.82 us

profile of v7, /device:TPU:0, one launch (start us, length us, event | category | flops | bytes accessed | tf_op | source)
XLA Modules:
  0.0 65.7 jit_solution(7535134230711209330)
XLA Ops:
  0.0 63.8 %layer.1 = bf16[1,32,7168]{2,1,0:T(8,128)(2,1)} custom-call(bf16[1,32,576]{2,1,0:T(8,128)(2,1)} %lat_in.1, f32[1,512]{1,0:T(1,128)} %gain_in.1, f32[2,144,128]{2,1,0:T(8,128)} %constant.2.clone.tables_in, s32[1,16]{1,0:T(1,128)} %order_in.1, bf16[1,256,1536]{2,1,0:T(8,128)(2,1)} %q_in.1, bf16[1,512,2048]{2,1,0:T(8,128)(2,1)} %up_in.1, ...), custom_call_target="tpu_custom_call" | custom-call | tf_op jit(solution)/shard_map/layer/pallas_call | solution.py:401
  63.8 1.8 %copy.10 = bf16[1,32,7168]{2,1,0:T(8,128)(2,1)} copy(bf16[1,32,7168]{2,1,0:T(8,128)(2,1)} %layer.1) | data formatting | bytes 917504
